TPU v7x, 128 devices: a whole 4x4x4 slice. The times are simulated.
128 devices in a mesh: ra: 32 (over y_lo, x, z), dec: 4 (over y_hi, core).
Axes of the slice: x: 4, y: 4 (y_hi: 2, y_lo: 2; y = y_hi * 2 + y_lo), z: 4, core: 2. Of those that a mesh axis runs over, the one named last changes fastest.
Arguments:
- lens_block: bfloat16 [32, 4, 130, 512], P('ra', 'dec'), may hold values from 0 to 255, as said below
- lens_count: int32 [32, 4], P('ra', 'dec'), may hold values from 64 to 512, as said below
- lens_region: int32 [32, 4, 512], P('ra', 'dec'), may hold values from 0 to 1023, as said below
- lens_sample: int32 [32, 4, 512], P('ra', 'dec'), may hold values from 0 to 7
- source_block: bfloat16 [32, 4, 133, 1024], P('ra', 'dec'), may hold values from -1 to 255, as said below
Outputs:
- jk_signal: float32 [1024, 8, 20], P(('ra', 'dec'))
- jk_weight: float32 [1024, 8, 20], P(('ra', 'dec'))
Inputs may be any that keep to these rules, and one draw needn't show every extreme that they name: The live lenses of patch (i, j) fill its first lens_count[i, j] slots; each count is 512, 256, 128 or 64, and at least one patch is full. `lens_block`: the first 128 rows are zero or positive, and zero below the lens's own redshift bin; the last two rows are whole numbers from 0 to 255. `source_block`: the first 128 rows are zero or positive; positions are whole numbers from 0 to 255; weights are positive. `lens_region`: each id labels a compact area of the sky.
All inputs are finite; a program needn't handle non-finite values.
Results may differ from a plain program's by a relative error of at most 0.0003.
Values may be sent and summed in bfloat16 or wider, within the bound.
No kernel may reach another device: no remote copies, remote signals or barrier semaphores. Data moves between devices by JAX's collectives and lax.ppermute only.
A program may use at most 64 MiB of HBM per device.

v0:
```python
import math

import jax
import jax.numpy as jnp
from jax import lax
from jax.sharding import PartitionSpec as P

NBIN = 20
SAMPLES = 8
PATCH = 256
R_IN = 12
L_PATCH = 512
S_PATCH = 1024
REG_DEV = 8


growth_top = 23
growth_bottom = 20


def extended(block, sides, width, periodic):
    for axis, dim in sides:
        count = lax.axis_size(axis)
        forward = [(i, i + 1) for i in range(count - 1)]
        if periodic:
            forward.append((count - 1, 0))
        backward = [(target, source) for source, target in forward]
        low = lax.ppermute(
            lax.slice_in_dim(block, block.shape[dim] - width, None, axis=dim), axis, forward
        )
        high = lax.ppermute(lax.slice_in_dim(block, 0, width, axis=dim), axis, backward)
        block = jnp.concatenate([low, block, high], axis=dim)
    return block


def edge_squares():
    return [
        float((R_IN * growth_top**edge_level // growth_bottom**edge_level) ** 2)
        for edge_level in range(NBIN + 1)
    ]


def bin_scales():
    edge_sq = edge_squares()
    lens_per_cell = L_PATCH / (SAMPLES * REG_DEV)
    density = S_PATCH / (PATCH * PATCH)
    expected = [
        math.pi * (edge_sq[edge_level + 1] - edge_sq[edge_level]) * density * lens_per_cell
        for edge_level in range(NBIN)
    ]
    return jnp.array(expected, jnp.float32)


def pair_sums(kernel_tile, lens_x, lens_y, source_rows, edge_sq):
    pdf_bins = kernel_tile.shape[0]
    inverse_crit = lax.dot_general(
        kernel_tile,
        source_rows[:pdf_bins],
        (((0,), (0,)), ((), ())),
        preferred_element_type=jnp.float32,
    )
    catalog = source_rows[pdf_bins:].astype(jnp.float32)
    delta_x = catalog[0][None, :] - lens_x[:, None]
    delta_y = catalog[1][None, :] - lens_y[:, None]
    radius_sq = delta_x * delta_x + delta_y * delta_y
    safe_sq = jnp.maximum(radius_sq, edge_sq[0])
    cos_two = (delta_x * delta_x - delta_y * delta_y) / safe_sq
    sin_two = 2.0 * delta_x * delta_y / safe_sq
    tangent = -(catalog[2][None, :] * cos_two + catalog[3][None, :] * sin_two)
    weighted = catalog[4][None, :] * inverse_crit
    signal = weighted * tangent
    weight = weighted * inverse_crit
    lower_sq = jnp.array(edge_sq[:-1], jnp.float32)[:, None, None]
    upper_sq = jnp.array(edge_sq[1:], jnp.float32)[:, None, None]
    inside = (radius_sq[None] >= lower_sq) & (radius_sq[None] < upper_sq)
    signal_bins = jnp.sum(jnp.where(inside, signal[None], 0.0), axis=2)
    weight_bins = jnp.sum(jnp.where(inside, weight[None], 0.0), axis=2)
    return jnp.stack([signal_bins, weight_bins], axis=0)


def local_terms(lens_tile, neighbours, edge_sq):
    pdf_bins = lens_tile.shape[0] - 2
    kernel_tile = lens_tile[:pdf_bins]
    lens_x = lens_tile[pdf_bins].astype(jnp.float32)
    lens_y = lens_tile[pdf_bins + 1].astype(jnp.float32)
    totals = jnp.zeros((2, len(edge_sq) - 1, lens_tile.shape[1]), jnp.float32)
    for shift_x in (-1, 0, 1):
        for shift_y in (-1, 0, 1):
            source_rows = neighbours[3 * (shift_x + 1) + shift_y + 1]
            totals = totals + pair_sums(
                kernel_tile,
                lens_x - shift_x * PATCH,
                lens_y - shift_y * PATCH,
                source_rows,
                edge_sq,
            )
    return totals


def source_plan(lenses, beside_all, edge_sq, tile_rows):
    lens_total = lenses.shape[1]
    neighbours = [beside_all[shift_x, shift_y] for shift_x in range(3) for shift_y in range(3)]

    def tile_step(tile_index, totals):
        first_lens = tile_index * tile_rows
        lens_tile = lax.dynamic_slice_in_dim(lenses, first_lens, tile_rows, 1)
        tile_terms = local_terms(lens_tile, neighbours, edge_sq)
        return lax.dynamic_update_slice_in_dim(totals, tile_terms, first_lens, 2)

    empty_sums = jnp.zeros((2, NBIN, lens_total), jnp.float32)
    return lax.fori_loop(0, lens_total // tile_rows, tile_step, empty_sums)


def on_device(lens_block, lens_count, lens_region, lens_sample, source_block):
    edge_sq = edge_squares()
    lenses = lens_block[0, 0]
    lens_total = lenses.shape[1]
    tile_rows = math.gcd(lens_total, 128)
    live_count = lens_count[0, 0]
    partial_rows = extended(source_block, (("dec", 1),), 1, False)
    beside_all = extended(partial_rows, (("ra", 0),), 1, True)
    totals = source_plan(lenses, beside_all, edge_sq, tile_rows)
    live_lens = jnp.arange(lens_total, dtype=jnp.int32) < live_count
    totals = jnp.where(live_lens[None, None, :], totals, 0.0)
    per_lens = jnp.transpose(totals.reshape(2 * NBIN, lens_total))
    segment = lens_region[0, 0] * SAMPLES + lens_sample[0, 0]
    regions_total = REG_DEV * lax.axis_size("ra") * lax.axis_size("dec")
    region_table = jax.ops.segment_sum(per_lens, segment, num_segments=regions_total * SAMPLES)
    region_table = region_table.reshape(regions_total, SAMPLES * 2 * NBIN)
    owned_rows = lax.psum_scatter(region_table, ("ra", "dec"), scatter_dimension=0, tiled=True)
    owned_rows = owned_rows.reshape(-1, SAMPLES, 2, NBIN)
    scales = bin_scales()
    return (owned_rows[:, :, 0, :] / jnp.sqrt(scales), owned_rows[:, :, 1, :] / scales)


def solution(mesh):
    placed = (
        P("ra", "dec", None, None),
        P("ra", "dec"),
        P("ra", "dec", None),
        P("ra", "dec", None),
        P("ra", "dec", None, None),
    )
    return jax.shard_map(
        on_device,
        mesh=mesh,
        in_specs=placed,
        out_specs=(P(("ra", "dec"), None, None), P(("ra", "dec"), None, None)),
        check_vma=False,
    )
```

profile of v0, /device:TPU:1, one launch (start us, length us, event | category | flops | bytes accessed | tf_op | source)
XLA Modules:
  0.0 404.9 jit_solution(9451843157732237948)
XLA Ops:
  7.3 6.3 %collective-permute-start = (bf16[1,1,133,1024]{3,2,1,0:T(8,128)(2,1)}, bf16[1,1,133,1024]{3,2,1,0:T(8,128)(2,1)S(1)}, u32[]{:S(2)}, u32[]{:S(2)}) collective-permute-start(bf16[1,1,133,1024]{3,2,1,0:T(8,128)(2,1)} %param.30), channel_id=1, source_target_pairs={{0,1},{1,2},{2,3},{4,5},{5,6},{6,7},{8,9},{9,10},{10,11},{12,13},{... | collective-permute-start | bytes 817160 | tf_op jit(solution)/shard_map/ppermute | solution.py:28
  13.6 1.9 collective-permute-start.1
  15.5 1.9 collective-permute-done
  18.1 1.7 constant_dynamic-update-slice_fusion.1
  19.8 3.4 collective-permute-done.1
  23.9 1.6 collective-permute-start.2
  25.5 4.4 %collective-permute-start.3 = (bf16[1,3,133,1024]{3,2,1,0:T(8,128)(2,1)}, bf16[1,3,133,1024]{3,2,1,0:T(8,128)(2,1)S(1)}, u32[]{:S(2)}, u32[]{:S(2)}) collective-permute-start(bf16[1,3,133,1024]{3,2,1,0:T(8,128)(2,1)} %constant_dynamic-update-slice_fusion), channel_id=1, source_target_pairs={{4,0},{8,4},{12,8},{16,12},{20,16},{24,20},{28,24},{32,28},{36,32}... | collective-permute-start | bytes 2451464 | tf_op jit(solution)/shard_map/ppermute | solution.py:31
  31.3 12.0 %collective-permute-done.2 = bf16[1,3,133,1024]{3,2,1,0:T(8,128)(2,1)S(1)} collective-permute-done((bf16[1,3,133,1024]{3,2,1,0:T(8,128)(2,1)}, bf16[1,3,133,1024]{3,2,1,0:T(8,128)(2,1)S(1)}, u32[]{:S(2)}, u32[]{:S(2)}) %collective-permute-start.2) | collective-permute-done | bytes 817184 | tf_op jit(solution)/shard_map/ppermute | solution.py:28
  43.5 184.3 %while.18 = (s32[]{:T(128)}, f32[2,20,512]{2,1,0:T(8,128)S(1)}, bf16[133,1024]{1,0:T(8,128)(2,1)S(1)}, bf16[130,512]{1,0:T(8,128)(2,1)S(1)}, bf16[133,1024]{1,0:...) while((s32[]{:T(128)}, f32[2,20,512]{2,1,0:T(8,128)S(1)}, ...), condition=%wide.region_19.20_spmd.clone.clone, body=%wide.region_0.19_spmd.sunk.clone.clone.sunk | while | flops 488462080 | bytes 35383924 | solution.py:111
  46.9 18.2 %select_reduce_fusion.20 = (f32[20,128]{1,0:T(8,128)S(1)}, f32[20,128]{1,0:T(8,128)S(1)}, f32[20,128]{1,0:T(8,128)S(1)}, f32[20,128]{1,0:T(8,128)S(1)}, f32[20,1...) fusion(f32[128,1024]{1,0:T(8,128)S(1)} %get-tuple-element.1218, ...), kind=kLoop, calls=%fused_computation.4.clone.1 | loop fusion | flops 73379840 | bytes 6373536 | tf_op jit(solution)/shard_map/while/body/eval_jaxpr/reduce_sum | solution.py:76
  66.7 22.7 %select_reduce_fusion.21 = (f32[20,128]{1,0:T(8,128)S(1)}, f32[20,128]{1,0:T(8,128)S(1)}, f32[20,128]{1,0:T(8,128)S(1)}, f32[20,128]{1,0:T(8,128)S(1)}, f32[20,1...) fusion(f32[128,1024]{1,0:T(8,128)S(1)} %get-tuple-element.1270,, ...), kind=kLoop, calls=%fused_computation.2.clone.1 | loop fusion | flops 91724800 | bytes 7966880 | tf_op jit(solution)/shard_map/while/body/eval_jaxpr/reduce_sum | solution.py:76
  90.0 0.8 multiply_multiply_fusion.24
  92.9 18.2 %select_reduce_fusion.20 = (f32[20,128]{1,0:T(8,128)S(1)}, f32[20,128]{1,0:T(8,128)S(1)}, f32[20,128]{1,0:T(8,128)S(1)}, f32[20,128]{1,0:T(8,128)S(1)}, f32[20,1...) fusion(f32[128,1024]{1,0:T(8,128)S(1)} %get-tuple-element.1218, ...), kind=kLoop, calls=%fused_computation.4.clone.1 | loop fusion | flops 73379840 | bytes 6373536 | tf_op jit(solution)/shard_map/while/body/eval_jaxpr/reduce_sum | solution.py:76
  111.5 0.8 multiply_multiply_fusion.28
  112.8 22.7 %select_reduce_fusion.21 = (f32[20,128]{1,0:T(8,128)S(1)}, f32[20,128]{1,0:T(8,128)S(1)}, f32[20,128]{1,0:T(8,128)S(1)}, f32[20,128]{1,0:T(8,128)S(1)}, f32[20,1...) fusion(f32[128,1024]{1,0:T(8,128)S(1)} %get-tuple-element.1270,, ...), kind=kLoop, calls=%fused_computation.2.clone.1 | loop fusion | flops 91724800 | bytes 7966880 | tf_op jit(solution)/shard_map/while/body/eval_jaxpr/reduce_sum | solution.py:76
  136.0 0.8 multiply_multiply_fusion.24
  139.0 18.2 %select_reduce_fusion.20 = (f32[20,128]{1,0:T(8,128)S(1)}, f32[20,128]{1,0:T(8,128)S(1)}, f32[20,128]{1,0:T(8,128)S(1)}, f32[20,128]{1,0:T(8,128)S(1)}, f32[20,1...) fusion(f32[128,1024]{1,0:T(8,128)S(1)} %get-tuple-element.1218, ...), kind=kLoop, calls=%fused_computation.4.clone.1 | loop fusion | flops 73379840 | bytes 6373536 | tf_op jit(solution)/shard_map/while/body/eval_jaxpr/reduce_sum | solution.py:76
  158.8 22.7 %select_reduce_fusion.21 = (f32[20,128]{1,0:T(8,128)S(1)}, f32[20,128]{1,0:T(8,128)S(1)}, f32[20,128]{1,0:T(8,128)S(1)}, f32[20,128]{1,0:T(8,128)S(1)}, f32[20,1...) fusion(f32[128,1024]{1,0:T(8,128)S(1)} %get-tuple-element.1270,, ...), kind=kLoop, calls=%fused_computation.2.clone.1 | loop fusion | flops 91724800 | bytes 7966880 | tf_op jit(solution)/shard_map/while/body/eval_jaxpr/reduce_sum | solution.py:76
  182.0 0.8 multiply_multiply_fusion.24
  185.0 18.2 %select_reduce_fusion.20 = (f32[20,128]{1,0:T(8,128)S(1)}, f32[20,128]{1,0:T(8,128)S(1)}, f32[20,128]{1,0:T(8,128)S(1)}, f32[20,128]{1,0:T(8,128)S(1)}, f32[20,1...) fusion(f32[128,1024]{1,0:T(8,128)S(1)} %get-tuple-element.1218, ...), kind=kLoop, calls=%fused_computation.4.clone.1 | loop fusion | flops 73379840 | bytes 6373536 | tf_op jit(solution)/shard_map/while/body/eval_jaxpr/reduce_sum | solution.py:76
  204.8 22.7 %select_reduce_fusion.21 = (f32[20,128]{1,0:T(8,128)S(1)}, f32[20,128]{1,0:T(8,128)S(1)}, f32[20,128]{1,0:T(8,128)S(1)}, f32[20,128]{1,0:T(8,128)S(1)}, f32[20,1...) fusion(f32[128,1024]{1,0:T(8,128)S(1)} %get-tuple-element.1270,, ...), kind=kLoop, calls=%fused_computation.2.clone.1 | loop fusion | flops 91724800 | bytes 7966880 | tf_op jit(solution)/shard_map/while/body/eval_jaxpr/reduce_sum | solution.py:76
  228.0 4.4 %scatter_custom_fusion = f32[8192,40]{1,0:T(8,128)} fusion(s32[512]{0:T(512)S(1)} %bitcast.293, f32[512,40]{1,0:T(8,128)S(1)} %copy.29, f32[]{:T(128)} %constant.109.clone.1), kind=kCustom, calls=%fused_computation.199 | custom fusion | flops 20480 | bytes 1310724 | tf_op jit(solution)/shard_map/scatter-add | solution.py:128
  232.4 4.6 %reshape.888 = f32[1024,320]{1,0:T(8,128)} reshape(f32[8192,40]{1,0:T(8,128)} %scatter_custom_fusion) | data formatting | bytes 2621440 | tf_op jit(solution)/shard_map/reshape | solution.py:129
  237.0 159.5 %all-reduce.3.cloned.1.call-done = f32[1024,320]{1,0:T(8,128)} async-done(((f32[1024,320]{1,0:T(8,128)}), f32[1024,320]{1,0:T(8,128)}) %all-reduce.3.cloned.1.call-update) | async-done | bytes 1310736
  (129 shorter events, 20.2 us)
Async XLA Ops:
  7.2 36.3 %copy-start.2 = (f32[20]{0:T(128)S(1)}, f32[20]{0:T(128)}, u32[]{:S(2)}) copy-start(f32[20]{0:T(128)} %constant.113.clone..sunk.19) | copy-start | bytes 244
  7.2 36.3 %copy-start.3 = (f32[20]{0:T(128)S(1)}, f32[20]{0:T(128)}, u32[]{:S(2)}) copy-start(f32[20]{0:T(128)} %constant.112.clone..sunk.19) | copy-start | bytes 244
  7.2 36.3 %copy-start = (bf16[1,1,133,1024]{3,2,1,0:T(8,128)(2,1)S(1)}, bf16[1,1,133,1024]{3,2,1,0:T(8,128)(2,1)}, u32[]{:S(2)}) copy-start(bf16[1,1,133,1024]{3,2,1,0:T(8,128)(2,1)} %param.30) | copy-start | bytes 817156
  7.2 36.3 %copy-start.1 = (bf16[1,1,130,512]{3,2,1,0:T(8,128)(2,1)S(1)}, bf16[1,1,130,512]{3,2,1,0:T(8,128)(2,1)}, u32[]{:S(2)}) copy-start(bf16[1,1,130,512]{3,2,1,0:T(8,128)(2,1)} %param.26) | copy-start | bytes 399364
  7.2 389.3 %all-reduce.3.cloned.1.call-start = ((), (), s32[]{:S(2)}) async-start(), calls=%async_computation | async-start | bytes 3145728
  7.3 10.1 %collective-permute-start = (bf16[1,1,133,1024]{3,2,1,0:T(8,128)(2,1)}, bf16[1,1,133,1024]{3,2,1,0:T(8,128)(2,1)S(1)}, u32[]{:S(2)}, u32[]{:S(2)}) collective-permute-start(bf16[1,1,133,1024]{3,2,1,0:T(8,128)(2,1)} %param.30), channel_id=1, source_target_pairs={{0,1},{1,2},{2,3},{4,5},{5,6},{6,7},{8,9},{9,10},{10,11},{12,13},{... | collective-permute-start | bytes 817160 | tf_op jit(solution)/shard_map/ppermute | solution.py:28
  13.6 9.6 %collective-permute-start.1 = (bf16[1,1,133,1024]{3,2,1,0:T(8,128)(2,1)}, bf16[1,1,133,1024]{3,2,1,0:T(8,128)(2,1)S(1)}, u32[]{:S(2)}, u32[]{:S(2)}) collective-permute-start(bf16[1,1,133,1024]{3,2,1,0:T(8,128)(2,1)} %param.30), channel_id=1, source_target_pairs={{1,0},{2,1},{3,2},{5,4},{6,5},{7,6},{9,8},{10,9},{11,10},{13,12},{... | collective-permute-start | bytes 817160 | tf_op jit(solution)/shard_map/ppermute | solution.py:31
  23.9 19.4 %collective-permute-start.2 = (bf16[1,3,133,1024]{3,2,1,0:T(8,128)(2,1)}, bf16[1,3,133,1024]{3,2,1,0:T(8,128)(2,1)S(1)}, u32[]{:S(2)}, u32[]{:S(2)}) collective-permute-start(bf16[1,3,133,1024]{3,2,1,0:T(8,128)(2,1)} %constant_dynamic-update-slice_fusion), channel_id=1, source_target_pairs={{0,4},{4,8},{8,12},{12,16},{16,20},{20,24},{24,28},{28,32},{32,36}... | collective-permute-start | bytes 2451464 | tf_op jit(solution)/shard_map/ppermute | solution.py:28
  25.5 17.8 %collective-permute-start.3 = (bf16[1,3,133,1024]{3,2,1,0:T(8,128)(2,1)}, bf16[1,3,133,1024]{3,2,1,0:T(8,128)(2,1)S(1)}, u32[]{:S(2)}, u32[]{:S(2)}) collective-permute-start(bf16[1,3,133,1024]{3,2,1,0:T(8,128)(2,1)} %constant_dynamic-update-slice_fusion), channel_id=1, source_target_pairs={{4,0},{8,4},{12,8},{16,12},{20,16},{24,20},{28,24},{32,28},{36,32}... | collective-permute-start | bytes 2451464 | tf_op jit(solution)/shard_map/ppermute | solution.py:31
  232.4 165.1 %copy-start.4 = (f32[20]{0:T(128)S(1)}, f32[20]{0:T(128)}, u32[]{:S(2)}) copy-start(f32[20]{0:T(128)} %constant.122) | copy-start | bytes 244
  232.4 165.1 %copy-start.5 = (f32[20]{0:T(128)S(1)}, f32[20]{0:T(128)}, u32[]{:S(2)}) copy-start(f32[20]{0:T(128)} %constant.120) | copy-start | bytes 244
Sparse Core Ops, SparseCore 0:
  237.1 159.3 all-reduce.2
where the time goes:
time: 405 us
  waiting for transfers between devices  177 us (44%)
  other arithmetic  170 us (42%)
  matrix products  18.2 us (4%)
  between operations  14.9 us (4%)
  starting transfers between devices  14.4 us (4%)
  local copies, waits for them, and re-layouts  9.54 us (2%)
    reduce_sum x8, other arithmetic, pair_sums(): signal_bins = jnp.sum(jnp.where(inside, signal[None], 0.0), axis=2)  164 us
    unnamed x2, waiting for transfers between devices  160 us
    dot_general x36, matrix products, pair_sums(): lax.dot_general(kernel_tile, source_rows[:pdf_bins], (((0,), (0,)), ((),...  18.2 us
    ppermute x2, waiting for transfers between devices, extended(): lax.ppermute(lax.slice_in_dim(block, block.shape[dim] - width, None, axis...  13.8 us
  transfers between devices with their start and end apart: 5, of which 4 were waited for; matrix products, arithmetic and copies ran while one was open for 1% of the time, Pallas kernels for 0%

commit v1 on v0

v1 whole, which is shorter than its diff:
```python
import functools
import math

import jax
import jax.numpy as jnp
import numpy as np
from jax import lax
from jax.experimental import pallas as pl
from jax.experimental.pallas import tpu as pltpu
from jax.sharding import PartitionSpec as P

NBIN = 20
SAMPLES = 8
PATCH = 256
R_IN = 12
L_PATCH = 512
S_PATCH = 1024
REG_DEV = 8
ZROWS = 128
LANES = 128
SUB = 8
SRC_TILES = S_PATCH // LANES
LENS_TILES = L_PATCH // SUB
UNROLL = 4
FAR = 1.0e6
BOX_ROW = ZROWS + 5
BLOCK_ROWS = 144
COUNT_LANE = 120
FOLD = 2
VMEM_MIB = 40
THRESHOLD_SUMS = 2 * (NBIN + 1)
growth_top = 23
growth_bottom = 20


def edge_squares():
    return [
        float((R_IN * growth_top**k // growth_bottom**k) ** 2) for k in range(NBIN + 1)
    ]


EDGES = edge_squares()
GROUPS = ((0, 10), (10, 16), (16, 21))


def bin_scales():
    lens_per_cell = L_PATCH / (SAMPLES * REG_DEV)
    density = S_PATCH / (PATCH * PATCH)
    expected = [
        math.pi * (EDGES[k + 1] - EDGES[k]) * density * lens_per_cell for k in range(NBIN)
    ]
    return jnp.array(expected, jnp.float32)


def tree_sum(terms):
    while len(terms) > 1:
        paired = [a + b for a, b in zip(terms[::2], terms[1::2])]
        terms = paired + ([terms[-1]] if len(terms) % 2 else [])
    return terms[0]


def spatial_order(x, y, dead, group):
    n = x.shape[0]
    index = jnp.arange(n, dtype=jnp.float32)
    key = x * n + index + dead * 2.0**20
    rank = jnp.sum((key[:, None] < key[None, :]).astype(jnp.float32), axis=0)
    key = jnp.floor(rank / group) * 2.0**18 + y * n + index
    return jnp.sum((key[:, None] < key[None, :]).astype(jnp.float32), axis=0)


def order_matrix(rank):
    n = rank.shape[0]
    target = lax.broadcasted_iota(jnp.float32, (n, n), 0)
    return (target == rank[None, :]).astype(jnp.bfloat16)


def tile_boxes(x, y):
    x, y = x.reshape(-1, LANES), y.reshape(-1, LANES)
    return jnp.stack([jnp.min(x, 1), jnp.max(x, 1), jnp.min(y, 1), jnp.max(y, 1)])


def tile_lists(columns_ref, boxes, valid, tiles, slots):
    wide = (LENS_TILES, LANES)

    def bound(row, reduce):
        column = columns_ref[:, ZROWS + row : ZROWS + row + 1]
        return reduce(column.reshape(LENS_TILES, SUB, 1), axis=1)

    gap_x = jnp.maximum(boxes[0] - bound(0, jnp.max), bound(0, jnp.min) - boxes[1])
    gap_y = jnp.maximum(boxes[2] - bound(1, jnp.max), bound(1, jnp.min) - boxes[3])
    gap_x, gap_y = jnp.maximum(gap_x, 0.0), jnp.maximum(gap_y, 0.0)
    near_sq = jnp.where(valid, gap_x * gap_x + gap_y * gap_y, FAR)
    upper = (
        (lax.broadcasted_iota(jnp.int32, (LANES, LANES), 0)
        <= lax.broadcasted_iota(jnp.int32, (LANES, LANES), 1)).astype(jnp.float32)
    ).astype(jnp.bfloat16)
    lane = lax.broadcasted_iota(jnp.int32, wide, 1)
    tile_id = lane.astype(jnp.float32) - tiles
    place = jnp.full(wide, -1.0, jnp.float32)
    base = jnp.zeros((LENS_TILES, 1), jnp.float32)
    listed = jnp.zeros(wide, jnp.float32)
    inner = jnp.zeros(wide, jnp.float32)
    for group, (_, hi) in enumerate(GROUPS):
        reach = (near_sq < EDGES[hi - 1]).astype(jnp.float32)
        member = reach - inner
        inner = reach
        running = jnp.dot(
            member.astype(jnp.bfloat16), upper, preferred_element_type=jnp.float32
        )
        place = jnp.where(member > 0.0, running + (base - 1.0), place)
        base = base + running[:, LANES - 1 :]
        listed = jnp.where(lane == COUNT_LANE + group, base - tiles, listed)
    for slot in range(slots):
        found = jnp.sum(jnp.where(place == float(slot), tile_id, 0.0), axis=1, keepdims=True)
        listed = jnp.where(lane == slot, found, listed)
    return (listed + tiles).astype(jnp.int32)


def pair_kernel(shifts, last, *refs):
    n = sum(len(group) for group in shifts)
    tiles = n * SRC_TILES
    live_ref, band_ref, columns_ref = refs[:3]
    blocks = refs[3 : 3 + len(shifts)]
    rest = refs[3 + len(shifts) :]
    if last:
        before_ref, out_ref, sums, *rest = rest
    else:
        before_ref, (sums, *rest) = None, rest
    crit, param, slots, list_vmem, list_ref, list_sem = rest
    live = live_ref[0]
    tile_shape = (SUB, LANES)
    patches = [
        (block, at, shift)
        for block, group in zip(blocks, shifts)
        for at, shift in enumerate(group)
    ]

    lane = lax.broadcasted_iota(jnp.int32, (1, LANES), 1)
    boxes = [jnp.zeros((1, LANES), jnp.float32) for _ in range(4)]
    valid = jnp.zeros((1, LANES), jnp.float32)
    for p, (block, at, shift) in enumerate(patches):
        own = (lane >= p * SRC_TILES) & (lane < (p + 1) * SRC_TILES)
        rows = block[at, BOX_ROW : BOX_ROW + 4, :LANES].astype(jnp.float32)
        rows = pltpu.roll(rows, p * SRC_TILES, axis=1)
        for c in range(4):
            boxes[c] = jnp.where(own, rows[c : c + 1] + shift[c // 2] * PATCH, boxes[c])
        there = band_ref[0] + shift[1]
        inside = ((there >= 0) & (there < band_ref[1])).astype(jnp.float32)
        valid = jnp.where(own, inside, valid)
    list_vmem[...] = tile_lists(
        columns_ref, boxes, valid > 0.0, tiles, -(-tiles // UNROLL) * UNROLL
    )
    copy = pltpu.make_async_copy(list_vmem, list_ref, list_sem)
    copy.start()

    for p, (block, at, (shift_x, shift_y)) in enumerate(patches):
        rows = block[at, ZROWS : ZROWS + 5, :].astype(jnp.float32)
        weight = rows[4:5]
        values = (
            rows[0:1] + shift_x * PATCH,
            rows[1:2] + shift_y * PATCH,
            -(weight * rows[2:3]),
            -2.0 * (weight * rows[3:4]),
            weight,
        )
        for t in range(SRC_TILES):
            for v, value in enumerate(values):
                param[p * SRC_TILES + t, v] = jnp.broadcast_to(
                    value[:, t * LANES : (t + 1) * LANES], tile_shape
                )
    for v in range(5):
        param[tiles, v] = jnp.full(tile_shape, FAR if v == 0 else 0.0, jnp.float32)
    crit[tiles] = jnp.zeros((L_PATCH, LANES), jnp.float32)

    def crit_step(chunk, carry):
        first = pl.multiple_of(chunk * LANES, LANES)
        kernel_rows = columns_ref[pl.ds(first, LANES), :ZROWS].astype(jnp.bfloat16)
        for p, (block, at, _) in enumerate(patches):
            product = jnp.dot(
                kernel_rows, block[at, :ZROWS, :], preferred_element_type=jnp.float32
            )
            for t in range(SRC_TILES):
                crit[p * SRC_TILES + t, pl.ds(first, LANES), :] = product[
                    :, t * LANES : (t + 1) * LANES
                ]
        return carry

    lax.fori_loop(0, (live + LANES - 1) // LANES, crit_step, 0)
    copy.wait()

    def gather(terms, carry, group):
        lo, hi = GROUPS[group]
        out = []
        for k in range(lo, hi):
            inside = [r2 < EDGES[k] for _, _, r2 in terms]
            for c in range(2):
                picked = [jnp.where(m, t[c], 0.0) for m, t in zip(inside, terms)]
                out.append(carry[2 * (k - lo) + c] + tree_sum(picked))
        return tuple(out)

    def lens_step(lens_tile, carry):
        first = pl.multiple_of(lens_tile * SUB, SUB)
        place = columns_ref[pl.ds(first, SUB), ZROWS : ZROWS + 2]
        lens_x = jnp.broadcast_to(place[:, 0:1], tile_shape)
        lens_y = jnp.broadcast_to(place[:, 1:2], tile_shape)

        def far_step(i, acc):
            terms = []
            for u in range(UNROLL):
                tile = list_ref[lens_tile, i * UNROLL + u]
                dx = param[tile, 0] - lens_x
                dy = param[tile, 1] - lens_y
                dx_sq, dy_sq = dx * dx, dy * dy
                r2 = dx_sq + dy_sq
                turned = param[tile, 2] * (dx_sq - dy_sq) + param[tile, 3] * (dx * dy)
                value = crit[tile, pl.ds(first, SUB), :]
                signal = value * (turned / jnp.maximum(r2, EDGES[0]))
                weight = param[tile, 4] * value * value
                slots[0, i * UNROLL + u] = signal
                slots[1, i * UNROLL + u] = weight
                slots[2, i * UNROLL + u] = r2
                terms.append((signal, weight, r2))
            return gather(terms, acc, 2)

        def near_step(group, i, acc):
            terms = [
                tuple(slots[c, i * UNROLL + u] for c in range(3)) for u in range(UNROLL)
            ]
            return gather(terms, acc, group)

        for group in (2, 1, 0):
            step = far_step if group == 2 else functools.partial(near_step, group)
            trips = (list_ref[lens_tile, COUNT_LANE + group] + UNROLL - 1) // UNROLL
            places = [
                c * (NBIN + 1) + k for k in range(*GROUPS[group]) for c in range(2)
            ]
            if before_ref is None:
                acc = (jnp.zeros(tile_shape, jnp.float32),) * len(places)
            else:
                acc = tuple(before_ref[lens_tile, v] for v in places)
            acc = lax.fori_loop(0, trips, step, acc)
            for v, value in zip(places, acc):
                sums[lens_tile, v] = value
        return carry

    lens_tiles = live // SUB
    lax.fori_loop(0, lens_tiles, lens_step, 0)

    if not last:
        return
    out_ref[...] = jnp.zeros_like(out_ref)

    lane = lax.broadcasted_iota(jnp.int32, tile_shape, 1)
    ones = jnp.ones((2 * LANES, LANES), jnp.bfloat16)

    def fold_step(step, carry):
        rows = (NBIN + 1) * SUB
        for u in range(FOLD):
            tile = step * FOLD + u
            total = jnp.zeros(tile_shape, jnp.float32)
            value = sums[tile, NBIN + 1 :].reshape(rows, LANES)
            high = value.astype(jnp.bfloat16)
            low = (value - high.astype(jnp.float32)).astype(jnp.bfloat16)
            both = jnp.concatenate([high, low], axis=1)
            folded = jnp.dot(both, ones, preferred_element_type=jnp.float32)
            for k in range(NBIN + 1):
                signal = jnp.sum(sums[tile, k], axis=1, keepdims=True)
                total = jnp.where(lane == k, signal, total)
                weight = folded[k * SUB : (k + 1) * SUB]
                total = jnp.where(lane == NBIN + 1 + k, weight, total)
            out_ref[pl.ds(pl.multiple_of(tile * SUB, SUB), SUB), :] = total
        return carry

    lax.fori_loop(0, lens_tiles // FOLD, fold_step, 0)


def pair_sums(live, bands, columns, blocks, shifts, before=None):
    n = sum(len(group) for group in shifts)
    tiles = n * SRC_TILES
    padded = -(-tiles // UNROLL) * UNROLL
    last = before is not None
    smem = pl.BlockSpec(memory_space=pltpu.SMEM)
    vmem = pl.BlockSpec(memory_space=pltpu.VMEM)
    all_sums = (LENS_TILES, THRESHOLD_SUMS, SUB, LANES)
    scratch = [
        pltpu.VMEM((tiles + 1, L_PATCH, LANES), jnp.float32),
        pltpu.VMEM((tiles + 1, 5, SUB, LANES), jnp.float32),
        pltpu.VMEM((3, padded, SUB, LANES), jnp.float32),
        pltpu.VMEM((LENS_TILES, LANES), jnp.int32),
        pltpu.SMEM((LENS_TILES, LANES), jnp.int32),
        pltpu.SemaphoreType.DMA,
    ]
    operands = (live, bands, columns, *blocks) + ((before,) if last else ())
    return pl.pallas_call(
        functools.partial(pair_kernel, shifts, last),
        out_shape=jax.ShapeDtypeStruct((L_PATCH, LANES) if last else all_sums, jnp.float32),
        in_specs=[smem] * 2 + [vmem] * (len(operands) - 2),
        out_specs=vmem,
        scratch_shapes=([pltpu.VMEM(all_sums, jnp.float32)] if last else []) + scratch,
        cost_estimate=pl.CostEstimate(
            flops=n * 20_000_000_000, transcendentals=0, bytes_accessed=n * 300_000
        ),
        compiler_params=pltpu.CompilerParams(vmem_limit_bytes=VMEM_MIB << 20),
        name=f"pairs_{n}",
    )(*operands)


WIDE = 3 * LANES


def split_parts(value):
    parts = []
    for _ in range(3):
        part = value.astype(jnp.bfloat16)
        value = value - part.astype(jnp.float32)
        parts.append(part)
    return parts


def bin_placement():
    matrix = np.zeros((LANES, WIDE), np.float32)
    for m in range(SAMPLES):
        for c in range(2):
            for k in range(NBIN):
                column = (m * 2 + c) * NBIN + k
                matrix[c * (NBIN + 1) + k + 1, column] = 1.0
                matrix[c * (NBIN + 1) + k, column] = -1.0
    return jnp.asarray(matrix, jnp.bfloat16)


def table_kernel(rows_ref, columns_ref, sums_ref, place_ref, out_ref):
    place = place_ref[...]
    parts = split_parts(sums_ref[...])
    bins = [jnp.dot(p, place, preferred_element_type=jnp.float32) for p in parts]
    bins = (bins[2] + bins[1]) + bins[0]
    sample = columns_ref[:, ZROWS + 4 : ZROWS + 5].astype(jnp.int32) * (2 * NBIN)
    lane = lax.broadcasted_iota(jnp.int32, bins.shape, 1) - sample
    bins = jnp.where((lane >= 0) & (lane < 2 * NBIN), bins, 0.0)
    region = (rows_ref[2:3] * 8.0 + rows_ref[3:4]).astype(jnp.int32)
    ids = lax.broadcasted_iota(jnp.int32, (out_ref.shape[0], region.shape[1]), 0)
    match = (ids == region).astype(jnp.float32).astype(jnp.bfloat16)
    sums = [jnp.dot(match, p, preferred_element_type=jnp.float32) for p in split_parts(bins)]
    out_ref[...] = (sums[2] + sums[1]) + sums[0]


def region_sums(rows, columns, per_lens, regions_total):
    vmem = pl.BlockSpec(memory_space=pltpu.VMEM)
    return pl.pallas_call(
        table_kernel,
        out_shape=jax.ShapeDtypeStruct((regions_total, WIDE), jnp.float32),
        in_specs=[vmem] * 4,
        out_specs=vmem,
        compiler_params=pltpu.CompilerParams(vmem_limit_bytes=32 << 20),
        name="region_table",
    )(rows, columns, per_lens, bin_placement())


def shifted(block, axis, periodic):
    count = lax.axis_size(axis)
    forward = [(i, i + 1) for i in range(count - 1)]
    if periodic:
        forward.append((count - 1, 0))
    backward = [(b, a) for a, b in forward]
    return lax.ppermute(block, axis, forward), lax.ppermute(block, axis, backward)


def on_device(lens_block, lens_count, lens_region, lens_sample, source_block):
    axes = ("ra", "dec")
    bands, band = lax.axis_size("dec"), lax.axis_index("dec")
    regions_total = REG_DEV * lax.axis_size("ra") * bands
    nothing = (((1,), (1,)), ((), ()))

    source = source_block[0, 0]
    source_rank = spatial_order(
        source[ZROWS].astype(jnp.float32), source[ZROWS + 1].astype(jnp.float32), 0.0, 256
    )
    source = lax.dot_general(
        source, order_matrix(source_rank), nothing, preferred_element_type=jnp.float32
    )
    boxes = tile_boxes(source[ZROWS], source[ZROWS + 1])
    boxes = jnp.pad(boxes, ((0, BLOCK_ROWS - BOX_ROW - 4), (0, S_PATCH - SRC_TILES)))
    source = jnp.concatenate([source, boxes], axis=0).astype(jnp.bfloat16)

    low, high = shifted(source, "ra", True)
    middle = jnp.stack([source, low, high])
    columns_at = (0, -1, 1)
    with jax.named_scope("halo_dec"):
        below, above = shifted(middle, "dec", False)

    lens = lens_block[0, 0]
    live = lens_count[0]
    dead = (jnp.arange(L_PATCH, dtype=jnp.int32) >= live[0]).astype(jnp.float32)
    lens_rank = spatial_order(
        lens[ZROWS].astype(jnp.float32), lens[ZROWS + 1].astype(jnp.float32), dead, 64
    )
    order = order_matrix(lens_rank)
    region, sample = lens_region[0], lens_sample[0]
    labels = jnp.concatenate([region // 8, region % 8, sample], axis=0).astype(jnp.bfloat16)
    lens = jnp.concatenate([lens, labels], axis=0)
    columns = lax.dot_general(order, lens, nothing, preferred_element_type=jnp.float32)
    rows = lax.dot_general(lens[ZROWS:], order, nothing, preferred_element_type=jnp.float32)
    where = jnp.stack([band, jnp.int32(bands)]).astype(jnp.int32)

    with jax.named_scope("pairs_near"):
        shifts = (tuple((a, 0) for a in columns_at),)
        near = pair_sums(live, where, columns, [middle], shifts)
    with jax.named_scope("pairs_far"):
        shifts = tuple(tuple((a, b) for a in columns_at) for b in (-1, 1))
        per_lens = pair_sums(live, where, columns, [below, above], shifts, near)

    table = region_sums(rows, columns, per_lens, regions_total)
    table = lax.all_to_all(table, axes, 0, 0, tiled=True)
    owned = jnp.sum(table.reshape(-1, REG_DEV, WIDE), axis=0)
    owned = owned[:, : 2 * NBIN * SAMPLES].reshape(REG_DEV, SAMPLES, 2, NBIN)
    scales = bin_scales()
    return (owned[:, :, 0, :] / jnp.sqrt(scales), owned[:, :, 1, :] / scales)


def solution(mesh):
    placed = (
        P("ra", "dec", None, None),
        P("ra", "dec"),
        P("ra", "dec", None),
        P("ra", "dec", None),
        P("ra", "dec", None, None),
    )
    return jax.shard_map(
        on_device,
        mesh=mesh,
        in_specs=placed,
        out_specs=(P(("ra", "dec"), None, None), P(("ra", "dec"), None, None)),
        check_vma=False,
    )
```

time: 405 us -> 113 us (0.28)
  waiting for transfers between devices: 177 us -> 6.22 us
  other arithmetic: 170 us -> 6.09 us
  blocking collectives: 0 us -> 47.2 us
  Pallas kernels: 0 us -> 30.6 us
  matrix products: 18.2 us -> 4.28 us
  between operations: 14.9 us -> 1.49 us
  local copies, waits for them, and re-layouts: 9.54 us -> 0.23 us
    reduce_sum x8 -> x5, other arithmetic: 164 us -> 1.48 us  [the longest x2 0.66 us: spatial_order(): return jnp.sum((key[:, None] < key[None, :]).astype(jnp.float32), axis=0)]
    unnamed x2 -> x0, waiting for transfers between devices: 160 us -> none
    all_to_all x0 -> x1, blocking collectives: none -> 47.2 us  [on_device(): table = lax.all_to_all(table, axes, 0, 0, tiled=True)]
    pallas_call x0 -> x3, Pallas kernels: none -> 30.6 us  [the longest x2 28.4 us: pair_sums(): pl.pallas_call(functools.partial(pair_kernel, shifts, last), out_shape=ja...]
    dot_general x36 -> x3, matrix products: 18.2 us -> 4.28 us  [the longest x1 1.99 us: on_device(): lax.dot_general(source, order_matrix(source_rank), nothing, preferred_ele...]
    ppermute x4, waiting for transfers between devices: 17.2 us -> 6.22 us  [the longest x2 6.14 us: shifted(): lax.ppermute(block, axis, forward)]
    reshape x3 -> x1, local copies, waits for them, and re-layouts: 4.77 us -> 0.15 us  [on_device(): owned = owned[:, :2 * NBIN * SAMPLES].reshape(REG_DEV, SAMPLES, 2, NBIN)]
    scatter-add x1 -> x0, other arithmetic: 4.4 us -> none  [on_device(): jax.ops.segment_sum(per_lens, segment, num_segments=regions_total * SAMPLES)]
  transfers between devices with their start and end apart: 5 -> 4, of which waited for: 4 -> 2; matrix products, arithmetic and copies ran while one was open for 1% -> 4% of each run, Pallas kernels for 0% -> 12%
where the time goes in v1:
time: 113 us; the launch traced here: 112 us
  blocking collectives  47.2 us (42%)
  Pallas kernels  30.6 us (27%)
  starting transfers between devices  16 us (14%)
  waiting for transfers between devices  6.22 us (6%)
  other arithmetic  6.09 us (5%)
  matrix products  4.28 us (4%)
  between operations  1.49 us (1%)
    all_to_all x1, blocking collectives, on_device(): table = lax.all_to_all(table, axes, 0, 0, tiled=True)  47.2 us
    pallas_call x2, Pallas kernels, pair_sums(): pl.pallas_call(functools.partial(pair_kernel, shifts, last), out_shape=ja...  28.4 us
    ppermute x2, starting transfers between devices, shifted(): lax.ppermute(block, axis, backward)  11.6 us
    ppermute x2, waiting for transfers between devices, shifted(): lax.ppermute(block, axis, forward)  6.14 us
    ppermute x2, starting transfers between devices, shifted(): lax.ppermute(block, axis, forward)  4.48 us
  transfers between devices with their start and end apart: 4, of which 2 were waited for; matrix products, arithmetic and copies ran while one was open for 4% of the time, Pallas kernels for 12%

profile of v1, /device:TPU:1, one launch (start us, length us, event | category | flops | bytes accessed | tf_op | source)
XLA Modules:
  0.0 112.1 jit_solution(8388074828942585982)
XLA Ops:
  0.6 0.8 convert_multiply_fusion.1
  1.5 0.5 convert_reduce_fusion.1
  1.9 0.5 convert_reduce_fusion
  2.4 2.0 %fusion.31 = (bf16[133,1024]{1,0:T(8,128)(2,1)S(1)}, f32[133,1024]{1,0:T(8,128)S(1)}) fusion(bf16[1,1,133,1024]{3,2,1,0:T(8,128)(2,1)} %param.11, f32[1024]{0:T(1024)S(1)} %convert_reduce_fusion), kind=kOutput, calls=%fused_computation.63 | convolution fusion | flops 280105984 | bytes 1093632 | tf_op jit(solution)/shard_map/dot_general | solution.py:377
  4.4 0.1 fusion.27
  4.7 7.8 %collective-permute-start.1 = (bf16[144,1024]{1,0:T(8,128)(2,1)S(1)}, bf16[144,1024]{1,0:T(8,128)(2,1)S(1)}, u32[]{:S(2)}, u32[]{:S(2)}) collective-permute-start(bf16[144,1024]{1,0:T(8,128)(2,1)S(1)} %pad_maximum_fusion.1), channel_id=1, source_target_pairs={{4,0},{8,4},{12,8},{16,12},{20,16},{24,20},{28,24},{32,28},{36,32}... | collective-permute-start | bytes 884744 | tf_op jit(solution)/shard_map/ppermute | solution.py:364
  13.2 0.7 convert_bitcast_fusion
  13.9 0.7 fusion.24
  14.6 0.8 convert_multiply_fusion.3
  15.4 0.2 convert_reduce_fusion.3
  15.6 0.2 convert_reduce_fusion.2
  15.7 1.0 fusion.4.rows_ref
  16.9 1.3 %fusion.3.refs_2_.columns_ref = f32[512,133]{1,0:T(8,128)S(1)} fusion(f32[512]{0:T(512)S(1)} %convert_reduce_fusion.2, bf16[1,512]{1,0:T(2,128)(2,1)S(1)} %convert_bitcast_fusion, bf16[1,512]{1,0:T(2,128)(2,1)S(1)} %fusion.23, bf16[1,512]{1,0:T(2,128)(2,1)S(1)} %get-tuple-element.6, bf16[130,512]{1,0:T(8,128)(2,1)} %bitcast.71), kind=kOutput, calls=%fused_computation.9 | convolution fusion | flops 70537216 | bytes 410624 | tf_op jit(solution)/shard_map/dot_general | solution.py:400
  18.2 6.1 %collective-permute-done = bf16[144,1024]{1,0:T(8,128)(2,1)S(1)} collective-permute-done((bf16[144,1024]{1,0:T(8,128)(2,1)S(1)}, bf16[144,1024]{1,0:T(8,128)(2,1)S(1)}, u32[]{:S(2)}, u32[]{:S(2)}) %collective-permute-start) | collective-permute-done | bytes 294944 | tf_op jit(solution)/shard_map/ppermute | solution.py:364
  24.4 3.7 %collective-permute-start.3 = (bf16[3,144,1024]{2,1,0:T(8,128)(2,1)S(1)}, bf16[3,144,1024]{2,1,0:T(8,128)(2,1)S(1)}, u32[]{:S(2)}, u32[]{:S(2)}) collective-permute-start(bf16[3,144,1024]{2,1,0:T(8,128)(2,1)S(1)} %pad_maximum_fusion.refs_3_), channel_id=1, source_target_pairs={{1,0},{2,1},{3,2},{5,4},{6,5},{7,6},{9,8},{10,9},{11,10},{13,12},{... | collective-permute-start | bytes 2654216 | tf_op jit(solution)/shard_map/halo_dec/ppermute | solution.py:364
  28.1 4.5 %collective-permute-start.2 = (bf16[3,144,1024]{2,1,0:T(8,128)(2,1)S(1)}, bf16[3,144,1024]{2,1,0:T(8,128)(2,1)S(1)}, u32[]{:S(2)}, u32[]{:S(2)}) collective-permute-start(bf16[3,144,1024]{2,1,0:T(8,128)(2,1)S(1)} %pad_maximum_fusion.refs_3_), channel_id=1, source_target_pairs={{0,1},{1,2},{2,3},{4,5},{5,6},{6,7},{8,9},{9,10},{10,11},{12,13},{... | collective-permute-start | bytes 2654216 | tf_op jit(solution)/shard_map/halo_dec/ppermute | solution.py:364
  32.6 13.4 %pairs_3.1.refs_5_ = f32[64,42,8,128]{3,2,1,0:T(8,128)S(1)} custom-call(s32[1]{0:T(128)} %bitcast.47.refs_0_, s32[2]{0:T(128)S(1)} %pad_add_fusion.refs_1_, f32[512,133]{1,0:T(8,128)S(1)} %fusion.3.refs_2_.columns_ref, bf16[3,144,1024]{2,1,0:T(8,128)(2,1)S(1)} %pad_maximum_fusion.refs_3_), custom_call_target="tpu_custom_call" | custom-call | flops 60000002048 | bytes 900000 | tf_op jit(solution)/shard_map/pairs_near/pairs_3/pallas_call | solution.py:294
  46.0 15.0 %pairs_6.1.sums_ref = f32[512,128]{1,0:T(8,128)S(1)} custom-call(s32[1]{0:T(128)} %bitcast.48.refs_0_, s32[2]{0:T(128)S(1)} %pad_add_fusion.refs_1_, f32[512,133]{1,0:T(8,128)S(1)} %fusion.3.refs_2_.columns_ref, bf16[3,144,1024]{2,1,0:T(8,128)(2,1)S(1)} %collective-permute-done.2.refs_3_, bf16[3,144,1024]{2,1,0:T(8,128)(2,1)S(1)} %collective-permute-done.3.refs_4_, ...), custom_call_target="tpu_custom_call" | custom-call | flops 120000004096 | bytes 1800000 | tf_op jit(solution)/shard_map/pairs_far/pairs_6/pallas_call | solution.py:294
  61.1 2.2 %region_table.1 = f32[1024,384]{1,0:T(8,128)S(1)} custom-call(f32[5,512]{1,0:T(8,128)S(1)} %fusion.4.rows_ref, f32[512,133]{1,0:T(8,128)S(1)} %fusion.3.refs_2_.columns_ref, f32[512,128]{1,0:T(8,128)S(1)} %pairs_6.1.sums_ref, bf16[128,384]{1,0:T(8,128)(2,1)S(1)} %copy-done), custom_call_target="tpu_custom_call" | custom-call | tf_op jit(solution)/shard_map/region_table/pallas_call | solution.py:348
  63.3 47.2 %all_to_all.9 = f32[128,8,384]{2,1,0:T(8,128)S(1)} all-to-all(f32[128,8,384]{2,1,0:T(8,128)S(1)} %bitcast.49), channel_id=1, replica_groups=mesh['ra'=32,'dec'=4] {'ra','dec'}, dimensions={0} | all-to-all | bytes 3145728 | tf_op jit(solution)/shard_map/all_to_all | solution.py:412
  110.5 0.2 reduce_sum.49
  110.7 0.1 reshape.322
  110.9 0.6 broadcast_multiply_fusion.1
  111.5 0.6 broadcast_multiply_fusion
  (22 shorter events, 0.4 us)
Async XLA Ops:
  4.7 13.5 %collective-permute-start.1 = (bf16[144,1024]{1,0:T(8,128)(2,1)S(1)}, bf16[144,1024]{1,0:T(8,128)(2,1)S(1)}, u32[]{:S(2)}, u32[]{:S(2)}) collective-permute-start(bf16[144,1024]{1,0:T(8,128)(2,1)S(1)} %pad_maximum_fusion.1), channel_id=1, source_target_pairs={{4,0},{8,4},{12,8},{16,12},{20,16},{24,20},{28,24},{32,28},{36,32}... | collective-permute-start | bytes 884744 | tf_op jit(solution)/shard_map/ppermute | solution.py:364
  12.5 11.8 %collective-permute-start = (bf16[144,1024]{1,0:T(8,128)(2,1)S(1)}, bf16[144,1024]{1,0:T(8,128)(2,1)S(1)}, u32[]{:S(2)}, u32[]{:S(2)}) collective-permute-start(bf16[144,1024]{1,0:T(8,128)(2,1)S(1)} %pad_maximum_fusion.1), channel_id=1, source_target_pairs={{0,4},{4,8},{8,12},{12,16},{16,20},{20,24},{24,28},{28,32},{32,36}... | collective-permute-start | bytes 884744 | tf_op jit(solution)/shard_map/ppermute | solution.py:364
  24.4 21.6 %collective-permute-start.3 = (bf16[3,144,1024]{2,1,0:T(8,128)(2,1)S(1)}, bf16[3,144,1024]{2,1,0:T(8,128)(2,1)S(1)}, u32[]{:S(2)}, u32[]{:S(2)}) collective-permute-start(bf16[3,144,1024]{2,1,0:T(8,128)(2,1)S(1)} %pad_maximum_fusion.refs_3_), channel_id=1, source_target_pairs={{1,0},{2,1},{3,2},{5,4},{6,5},{7,6},{9,8},{10,9},{11,10},{13,12},{... | collective-permute-start | bytes 2654216 | tf_op jit(solution)/shard_map/halo_dec/ppermute | solution.py:364
  28.1 17.9 %collective-permute-start.2 = (bf16[3,144,1024]{2,1,0:T(8,128)(2,1)S(1)}, bf16[3,144,1024]{2,1,0:T(8,128)(2,1)S(1)}, u32[]{:S(2)}, u32[]{:S(2)}) collective-permute-start(bf16[3,144,1024]{2,1,0:T(8,128)(2,1)S(1)} %pad_maximum_fusion.refs_3_), channel_id=1, source_target_pairs={{0,1},{1,2},{2,3},{4,5},{5,6},{6,7},{8,9},{9,10},{10,11},{12,13},{... | collective-permute-start | bytes 2654216 | tf_op jit(solution)/shard_map/halo_dec/ppermute | solution.py:364
  46.0 15.0 %copy-start = (bf16[128,384]{1,0:T(8,128)(2,1)S(1)}, bf16[128,384]{1,0:T(8,128)(2,1)}, u32[]{:S(2)}) copy-start(bf16[128,384]{1,0:T(8,128)(2,1)} %constant.62.clone.place_ref) | copy-start | bytes 294916
  61.0 49.9 %copy-start.2 = (f32[20]{0:T(128)S(1)}, f32[20]{0:T(128)}, u32[]{:S(2)}) copy-start(f32[20]{0:T(128)} %constant.71) | copy-start | bytes 244
  61.1 50.5 %copy-start.1 = (f32[20]{0:T(128)S(1)}, f32[20]{0:T(128)}, u32[]{:S(2)}) copy-start(f32[20]{0:T(128)} %constant.73) | copy-start | bytes 244

commit v2 on v1

v2 whole, which is shorter than its diff:
```python
import functools
import math

import jax
import jax.numpy as jnp
import numpy as np
from jax import lax
from jax.experimental import pallas as pl
from jax.experimental.pallas import tpu as pltpu
from jax.sharding import PartitionSpec as P

NBIN = 20
SAMPLES = 8
PATCH = 256
R_IN = 12
L_PATCH = 512
S_PATCH = 1024
REG_DEV = 8
ZROWS = 128
LANES = 128
SUB = 8
SRC_TILES = S_PATCH // LANES
LENS_TILES = L_PATCH // SUB
UNROLL = (4, 4, 4)
CRIT_ROW = 5 * SUB
FAR = 1.0e6
BOX_ROW = ZROWS + SUB
BLOCK_ROWS = 144
LIST_WORDS = 16
FOLD_SPLIT = 22
VMEM_MIB = 26
THRESHOLD_SUMS = 2 * (NBIN + 1)
WIDE = 3 * LANES
growth_top = 23
growth_bottom = 20


def edge_squares():
    return [
        float((R_IN * growth_top**k // growth_bottom**k) ** 2) for k in range(NBIN + 1)
    ]


EDGES = edge_squares()
GROUPS = ((0, 10), (10, 16), (16, 21))


def bin_scales():
    lens_per_cell = L_PATCH / (SAMPLES * REG_DEV)
    density = S_PATCH / (PATCH * PATCH)
    expected = [
        math.pi * (EDGES[k + 1] - EDGES[k]) * density * lens_per_cell for k in range(NBIN)
    ]
    return jnp.array(expected, jnp.float32)


def tree_sum(terms):
    while len(terms) > 1:
        paired = [a + b for a, b in zip(terms[::2], terms[1::2])]
        terms = paired + ([terms[-1]] if len(terms) % 2 else [])
    return terms[0]


def spatial_order(x, y, dead, group):
    n = x.shape[0]
    index = jnp.arange(n, dtype=jnp.float32)
    key = x * n + index + dead * 2.0**20
    rank = jnp.sum((key[:, None] < key[None, :]).astype(jnp.float32), axis=0)
    key = jnp.floor(rank / group) * 2.0**18 + y * n + index
    return jnp.sum((key[:, None] < key[None, :]).astype(jnp.float32), axis=0)


def order_matrix(rank):
    n = rank.shape[0]
    target = lax.broadcasted_iota(jnp.float32, (n, n), 0)
    return (target == rank[None, :]).astype(jnp.bfloat16)


def tile_boxes(x, y):
    x, y = x.reshape(-1, LANES), y.reshape(-1, LANES)
    return jnp.stack([jnp.min(x, 1), jnp.max(x, 1), jnp.min(y, 1), jnp.max(y, 1)])


def tile_lists(lens_box, boxes, valid, tiles):
    wide = (tiles, LANES)
    gap_x = jnp.maximum(boxes[0] - lens_box[1:2], lens_box[0:1] - boxes[1])
    gap_y = jnp.maximum(boxes[2] - lens_box[3:4], lens_box[2:3] - boxes[3])
    gap_x, gap_y = jnp.maximum(gap_x, 0.0), jnp.maximum(gap_y, 0.0)
    near_sq = jnp.where(valid, gap_x * gap_x + gap_y * gap_y, FAR)
    lower = lax.broadcasted_iota(jnp.int32, (tiles, tiles), 0)
    lower = (lower >= lax.broadcasted_iota(jnp.int32, (tiles, tiles), 1)).astype(jnp.float32)
    lower = lower.astype(jnp.bfloat16)
    tile_id = lax.broadcasted_iota(jnp.int32, wide, 0).astype(jnp.float32) - tiles
    place = jnp.full(wide, -1.0, jnp.float32)
    base = jnp.zeros((1, LANES), jnp.float32)
    inner = jnp.zeros(wide, jnp.float32)
    trips = []
    for group, (_, hi) in enumerate(GROUPS):
        reach = (near_sq < EDGES[hi - 1]).astype(jnp.float32)
        member = (reach - inner).astype(jnp.bfloat16)
        running = jnp.dot(lower, member, preferred_element_type=jnp.float32)
        place = jnp.where(reach > inner, running + (base - 1.0), place)
        inner = reach
        base = base + running[tiles - 1 :]
        trips.append(jnp.floor((base + (UNROLL[group] - 1)) * (1.0 / UNROLL[group])))
    partial = []
    for slot in range(tiles):
        hit = jnp.where(place == float(slot), tile_id, 0.0)
        partial.append(tree_sum([hit[r : r + SUB] for r in range(0, tiles, SUB)]))
    partial = jnp.concatenate(partial, axis=0).astype(jnp.bfloat16)
    words = LIST_WORDS
    row = lax.broadcasted_iota(jnp.int32, (2 * words, tiles * SUB), 0)
    slot = lax.broadcasted_iota(jnp.int32, (2 * words, tiles * SUB), 1) >> 3
    first = 4 * (row & (words - 1)) + 2 * (row >> 4)
    take = jnp.where(slot == first, 1.0, jnp.where(slot == first + 1, 128.0, 0.0))
    packed = jnp.dot(take.astype(jnp.bfloat16), partial, preferred_element_type=jnp.float32)
    packed = (packed + 129.0 * tiles).astype(jnp.int32)
    packed = packed[:words] + packed[words:] * (1 << 14)
    row = lax.broadcasted_iota(jnp.int32, (SUB, LANES), 0)
    counts = jnp.where(row == 0, trips[0], jnp.where(row == 1, trips[1], trips[2]))
    return jnp.concatenate([packed, counts.astype(jnp.int32)], axis=0)


def pair_kernel(shifts, later, last, *refs):
    n = sum(len(group) for group in shifts)
    tiles = n * SRC_TILES
    live_ref, band_ref, columns_ref, place_ref, box_ref = refs[:5]
    blocks = refs[5 : 5 + len(shifts)]
    rest = refs[5 + len(shifts) :]
    before_ref = None
    if later:
        before_ref, *rest = rest
    if last:
        fold_ref, out_ref, *rest = rest
    sums, *rest = rest
    tables, slots, list_vmem, list_ref, list_sem = rest
    live = live_ref[0]
    tile_shape = (SUB, LANES)
    patches = [
        (block, at, shift)
        for block, group in zip(blocks, shifts)
        for at, shift in enumerate(group)
    ]

    boxes, valid = [[] for _ in range(4)], []
    for block, at, shift in patches:
        for c in range(4):
            part = block[at, BOX_ROW : BOX_ROW + SUB, c * LANES : (c + 1) * LANES]
            boxes[c].append(part.astype(jnp.float32) + shift[c // 2] * PATCH)
        there = band_ref[0] + shift[1]
        inside = (there >= 0) & (there < band_ref[1])
        valid.append(jnp.full(tile_shape, inside.astype(jnp.float32)))
    boxes = [jnp.concatenate(box, axis=0) for box in boxes]
    valid = jnp.concatenate(valid, axis=0) > 0.0
    list_vmem[...] = tile_lists(box_ref[...], boxes, valid, tiles)
    copy = pltpu.make_async_copy(list_vmem, list_ref, list_sem)
    copy.start()

    for p, (block, at, (shift_x, shift_y)) in enumerate(patches):
        rows = block[at, ZROWS : ZROWS + 5, :].astype(jnp.float32)
        weight = rows[4:5]
        values = (
            rows[0:1] + shift_x * PATCH,
            rows[1:2] + shift_y * PATCH,
            -(weight * rows[2:3]),
            -2.0 * (weight * rows[3:4]),
            weight,
        )
        for t in range(SRC_TILES):
            for v, value in enumerate(values):
                tables[p * SRC_TILES + t, v * SUB : (v + 1) * SUB] = jnp.broadcast_to(
                    value[:, t * LANES : (t + 1) * LANES], tile_shape
                )
    for v in range(5):
        tables[tiles, v * SUB : (v + 1) * SUB] = jnp.full(
            tile_shape, FAR if v == 0 else 0.0, jnp.float32
        )
    tables[tiles, CRIT_ROW:] = jnp.zeros((L_PATCH, LANES), jnp.float32)

    def crit_step(chunk, carry):
        first = pl.multiple_of(chunk * LANES, LANES)
        kernel_rows = columns_ref[pl.ds(first, LANES), :ZROWS].astype(jnp.bfloat16)
        for p, (block, at, _) in enumerate(patches):
            product = jnp.dot(
                kernel_rows, block[at, :ZROWS, :], preferred_element_type=jnp.float32
            )
            for t in range(SRC_TILES):
                tables[p * SRC_TILES + t, pl.ds(CRIT_ROW + first, LANES), :] = product[
                    :, t * LANES : (t + 1) * LANES
                ]
        return carry

    lax.fori_loop(0, (live + LANES - 1) // LANES, crit_step, 0)
    copy.wait()

    def add_up(rows, terms, group):
        for k in range(*GROUPS[group]):
            inside = [r2 < EDGES[k] for _, _, r2 in terms]
            for c in range(2):
                picked = [jnp.where(m, t[c], 0.0) for m, t in zip(inside, terms)]
                at = c * (NBIN + 1) + k
                sums[at, rows, :] = sums[at, rows, :] + tree_sum(picked)

    def lens_step(lens_tile, base):
        first = pl.multiple_of(lens_tile * SUB, SUB)
        rows = pl.ds(pl.multiple_of(first - base, SUB), SUB)
        trips = [list_ref[LIST_WORDS + group, lens_tile] for group in range(3)]
        lens_x = place_ref[0, pl.ds(first, SUB), :]
        lens_y = place_ref[1, pl.ds(first, SUB), :]
        for v in range(THRESHOLD_SUMS):
            sums[v, rows, :] = (
                before_ref[v, pl.ds(first, SUB), :] if later else jnp.zeros(tile_shape, jnp.float32)
            )

        def far_step(i, word):
            following = list_ref[i + 1, lens_tile]
            terms = []
            for u in range(4):
                tile = (word >> (7 * u)) & 127
                dx, dy = tables[tile, 0:SUB] - lens_x, tables[tile, SUB : 2 * SUB] - lens_y
                dx_sq, dy_sq = dx * dx, dy * dy
                r2 = dx_sq + dy_sq
                turned = tables[tile, 2 * SUB : 3 * SUB] * (dx_sq - dy_sq)
                turned = turned + tables[tile, 3 * SUB : 4 * SUB] * (dx * dy)
                value = tables[tile, pl.ds(CRIT_ROW + first, SUB), :]
                signal = value * (turned / jnp.maximum(r2, EDGES[0]))
                weight = tables[tile, 4 * SUB : 5 * SUB] * value * value
                slots[0, i * UNROLL[2] + u] = signal
                slots[1, i * UNROLL[2] + u] = weight
                slots[2, i * UNROLL[2] + u] = r2
                terms.append((signal, weight, r2))
            add_up(rows, terms, 2)
            return following

        lax.fori_loop(0, trips[2], far_step, list_ref[0, lens_tile])
        for group in (1, 0):

            def near_step(i, nothing, group=group):
                terms = [
                    tuple(slots[c, i * UNROLL[group] + u] for c in range(3))
                    for u in range(UNROLL[group])
                ]
                add_up(rows, terms, group)
                return nothing

            lax.fori_loop(0, trips[group], near_step, 0)
        return base

    lens_tiles = live // SUB
    if not last:
        lax.fori_loop(0, lens_tiles, lens_step, 0)
        return
    out_ref[...] = jnp.zeros_like(out_ref)

    def chunk_step(chunk, carry):
        first = pl.multiple_of(chunk * LANES, LANES)
        tiles_first = chunk * (LANES // SUB)
        tiles_end = jnp.minimum(tiles_first + LANES // SUB, lens_tiles)
        lax.fori_loop(tiles_first, tiles_end, lens_step, first)
        high, low = [], []
        for v in range(THRESHOLD_SUMS):
            value = sums[v]
            high.append(value.astype(jnp.bfloat16))
            low.append((value - high[v].astype(jnp.float32)).astype(jnp.bfloat16))
        folded = []
        for lo, hi in ((0, FOLD_SPLIT), (FOLD_SPLIT, THRESHOLD_SUMS)):
            both = [jnp.concatenate(part[lo:hi], axis=1) for part in (high, low)]
            weights = fold_ref[lo * LANES : hi * LANES, :]
            folded += [jnp.dot(p, weights, preferred_element_type=jnp.float32) for p in both]
        folded = tree_sum(folded)
        row = lax.broadcasted_iota(jnp.int32, (LANES, LANES), 0) + first
        folded = jnp.where(row < live, folded, 0.0)
        out_ref[pl.ds(first, LANES), :] = folded
        return carry

    lax.fori_loop(0, (live + LANES - 1) // LANES, chunk_step, 0)


def fold_matrix():
    matrix = np.zeros((THRESHOLD_SUMS, LANES, LANES), np.float32)
    for v in range(THRESHOLD_SUMS):
        matrix[v, :, v] = 1.0
    return jnp.asarray(matrix.reshape(-1, LANES), jnp.bfloat16)


def pair_sums(live, bands, columns, place, lens_box, blocks, shifts, before=None, last=False):
    n = sum(len(group) for group in shifts)
    tiles = n * SRC_TILES
    later = before is not None
    smem = pl.BlockSpec(memory_space=pltpu.SMEM)
    vmem = pl.BlockSpec(memory_space=pltpu.VMEM)
    all_sums = (THRESHOLD_SUMS, L_PATCH, LANES)
    scratch = [
        pltpu.VMEM((tiles + 1, CRIT_ROW + L_PATCH, LANES), jnp.float32),
        pltpu.VMEM((3, tiles, SUB, LANES), jnp.float32),
        pltpu.VMEM((LIST_WORDS + SUB, LANES), jnp.int32),
        pltpu.SMEM((LIST_WORDS + SUB, LANES), jnp.int32),
        pltpu.SemaphoreType.DMA,
    ]
    operands = (live, bands, columns, place, lens_box, *blocks)
    operands += (before,) if later else ()
    operands += (fold_matrix(),) if last else ()
    return pl.pallas_call(
        functools.partial(pair_kernel, shifts, later, last),
        out_shape=jax.ShapeDtypeStruct((L_PATCH, LANES) if last else all_sums, jnp.float32),
        in_specs=[smem] * 2 + [vmem] * (len(operands) - 2),
        out_specs=vmem,
        input_output_aliases={5 + len(blocks): 0} if later and not last else {},
        scratch_shapes=([pltpu.VMEM((THRESHOLD_SUMS, LANES, LANES), jnp.float32)] if last else []) + scratch,
        cost_estimate=pl.CostEstimate(
            flops=n * 20_000_000_000, transcendentals=0, bytes_accessed=n * 300_000
        ),
        compiler_params=pltpu.CompilerParams(vmem_limit_bytes=VMEM_MIB << 20),
        name=f"pairs_{n}",
    )(*operands)


def split_parts(value):
    parts = []
    for _ in range(3):
        part = value.astype(jnp.bfloat16)
        value = value - part.astype(jnp.float32)
        parts.append(part)
    return parts


def bin_placement():
    matrix = np.zeros((LANES, WIDE), np.float32)
    for m in range(SAMPLES):
        for c in range(2):
            for k in range(NBIN):
                column = (m * 2 + c) * NBIN + k
                matrix[c * (NBIN + 1) + k + 1, column] = 1.0
                matrix[c * (NBIN + 1) + k, column] = -1.0
    return jnp.asarray(matrix, jnp.bfloat16)


def table_kernel(region_ref, sample_ref, sums_ref, place_ref, out_ref):
    def product(matrices, others):
        terms = [
            jnp.dot(a, b, preferred_element_type=jnp.float32) for a, b in zip(matrices, others)
        ]
        return (terms[2] + terms[1]) + terms[0]

    bins = product(split_parts(sums_ref[...]), [place_ref[...]] * 3)
    lane = lax.broadcasted_iota(jnp.int32, bins.shape, 1) - sample_ref[...] * (2 * NBIN)
    bins = jnp.where((lane >= 0) & (lane < 2 * NBIN), bins, 0.0)
    region = region_ref[...]
    ids = lax.broadcasted_iota(jnp.int32, (out_ref.shape[0], region.shape[1]), 0)
    match = (ids == region).astype(jnp.float32).astype(jnp.bfloat16)
    out_ref[...] = product([match] * 3, split_parts(bins))


def region_sums(region, sample, sums, regions_total):
    vmem = pl.BlockSpec(memory_space=pltpu.VMEM)
    return pl.pallas_call(
        table_kernel,
        out_shape=jax.ShapeDtypeStruct((regions_total, WIDE), jnp.float32),
        in_specs=[vmem] * 4,
        out_specs=vmem,
        compiler_params=pltpu.CompilerParams(vmem_limit_bytes=VMEM_MIB << 20),
        name="region_table",
    )(region, sample, sums, bin_placement())


def shifted(block, axis, periodic):
    count = lax.axis_size(axis)
    forward = [(i, i + 1) for i in range(count - 1)]
    if periodic:
        forward.append((count - 1, 0))
    backward = [(b, a) for a, b in forward]
    return lax.ppermute(block, axis, forward), lax.ppermute(block, axis, backward)


def on_device(lens_block, lens_count, lens_region, lens_sample, source_block):
    axes = ("ra", "dec")
    bands, band = lax.axis_size("dec"), lax.axis_index("dec")
    regions_total = REG_DEV * lax.axis_size("ra") * bands
    nothing = (((1,), (1,)), ((), ()))

    source = source_block[0, 0]
    source_rank = spatial_order(
        source[ZROWS].astype(jnp.float32), source[ZROWS + 1].astype(jnp.float32), 0.0, 256
    )
    source = lax.dot_general(
        source, order_matrix(source_rank), nothing, preferred_element_type=jnp.float32
    )
    boxes = tile_boxes(source[ZROWS], source[ZROWS + 1])
    boxes = jnp.broadcast_to(boxes.T[:, :, None], (SRC_TILES, 4, LANES)).reshape(SRC_TILES, -1)
    boxes = jnp.pad(boxes, ((BOX_ROW - ZROWS - 5, 0), (0, S_PATCH - 4 * LANES)))
    source = jnp.concatenate([source, boxes], axis=0).astype(jnp.bfloat16)

    low, high = shifted(source, "ra", True)
    middle = jnp.stack([source, low, high])
    columns_at = (0, -1, 1)
    with jax.named_scope("halo_dec"):
        below, above = shifted(middle, "dec", False)

    lens = lens_block[0, 0]
    live = lens_count[0]
    dead = (jnp.arange(L_PATCH, dtype=jnp.int32) >= live[0]).astype(jnp.float32)
    lens_rank = spatial_order(
        lens[ZROWS].astype(jnp.float32), lens[ZROWS + 1].astype(jnp.float32), dead, 64
    )
    order = order_matrix(lens_rank)
    region, sample = lens_region[0], lens_sample[0]
    labels = jnp.concatenate([region // 8, region % 8, sample], axis=0).astype(jnp.bfloat16)
    lens = jnp.concatenate([lens, labels], axis=0)
    columns = lax.dot_general(order, lens, nothing, preferred_element_type=jnp.float32)
    labels = columns[:, ZROWS + 2 :]
    region = (labels[:, 0] * 8.0 + labels[:, 1]).astype(jnp.int32)[None, :]
    sample = labels[:, 2:].astype(jnp.int32)
    place = columns[:, ZROWS : ZROWS + 2]
    wide = jnp.broadcast_to(place.T[:, :, None], (2, L_PATCH, LANES))
    place = place.reshape(LENS_TILES, SUB, 2)
    lens_box = jnp.stack([jnp.min(place, axis=1), jnp.max(place, axis=1)], axis=2)
    lens_box = jnp.pad(lens_box.reshape(LENS_TILES, 4).T, ((0, SUB - 4), (0, LANES - LENS_TILES)))
    where = jnp.stack([band, jnp.int32(bands)]).astype(jnp.int32)

    def pairs(blocks, shifts, before=None, last=False):
        return pair_sums(live, where, columns, wide, lens_box, blocks, shifts, before, last)

    sums = pairs([middle], (tuple((a, 0) for a in columns_at),))
    shifts = tuple(tuple((a, b) for a in columns_at) for b in (-1, 1))
    sums = pairs([below, above], shifts, sums, True)

    table = region_sums(region, sample, sums, regions_total)
    table = lax.all_to_all(table, axes, 0, 0, tiled=True)
    owned = jnp.sum(table.reshape(-1, REG_DEV, WIDE), axis=0)
    owned = owned[:, : 2 * NBIN * SAMPLES].reshape(REG_DEV, SAMPLES, 2, NBIN)
    scales = bin_scales()
    return (owned[:, :, 0, :] / jnp.sqrt(scales), owned[:, :, 1, :] / scales)


def solution(mesh):
    placed = (
        P("ra", "dec", None, None),
        P("ra", "dec"),
        P("ra", "dec", None),
        P("ra", "dec", None),
        P("ra", "dec", None, None),
    )
    return jax.shard_map(
        on_device,
        mesh=mesh,
        in_specs=placed,
        out_specs=(P(("ra", "dec"), None, None), P(("ra", "dec"), None, None)),
        check_vma=False,
    )
```

time: 113 us -> 98.4 us (0.87)
  Pallas kernels: 30.6 us -> 22.4 us
  blocking collectives: 47.2 us -> 40 us
  waiting for transfers between devices: 6.22 us -> 9.71 us
  matrix products: 4.28 us -> 2.39 us
  other arithmetic: 6.09 us -> 4.2 us
    pallas_call x2, Pallas kernels: 28.4 us -> 20.1 us  [pair_sums(): pl.pallas_call(functools.partial(pair_kernel, shifts, later, last), out_s...]
    all_to_all x1, blocking collectives: 47.2 us -> 40 us  [on_device(): table = lax.all_to_all(table, axes, 0, 0, tiled=True)]
    ppermute x2, waiting for transfers between devices: 0.08 us -> 3.44 us  [shifted(): lax.ppermute(block, axis, backward)]
  transfers between devices with their start and end apart: 4 -> 4, of which waited for: 2 -> 3; matrix products, arithmetic and copies ran while one was open for 4% -> 2% of each run, Pallas kernels for 12% -> 10%
where the time goes in v2:
time: 98.4 us; the launch traced here: 97.2 us
  blocking collectives  40 us (41%)
  Pallas kernels  22.4 us (23%)
  starting transfers between devices  16 us (16%)
  waiting for transfers between devices  9.71 us (10%)
  other arithmetic  4.2 us (4%)
  matrix products  2.39 us (2%)
  between operations  1.63 us (2%)
    all_to_all x1, blocking collectives, on_device(): table = lax.all_to_all(table, axes, 0, 0, tiled=True)  40 us
    pallas_call x2, Pallas kernels, pair_sums(): pl.pallas_call(functools.partial(pair_kernel, shifts, later, last), out_s...  20.1 us
    ppermute x2, starting transfers between devices, shifted(): lax.ppermute(block, axis, backward)  11.6 us
    ppermute x2, waiting for transfers between devices, shifted(): lax.ppermute(block, axis, forward)  6.27 us
    ppermute x2, starting transfers between devices, shifted(): lax.ppermute(block, axis, forward)  4.48 us
    ppermute x2, waiting for transfers between devices, shifted(): lax.ppermute(block, axis, backward)  3.44 us
    pallas_call x1, Pallas kernels, region_sums(): pl.pallas_call(table_kernel, out_shape=jax.ShapeDtypeStruct((regions_tota...  2.24 us
    dot_general x1, matrix products, on_device(): lax.dot_general(source, order_matrix(source_rank), nothing, preferred_ele...  1.99 us
  transfers between devices with their start and end apart: 4, of which 3 were waited for; matrix products, arithmetic and copies ran while one was open for 2% of the time, Pallas kernels for 10%

profile of v2, /device:TPU:1, one launch (start us, length us, event | category | flops | bytes accessed | tf_op | source)
XLA Modules:
  0.0 97.2 jit_solution(5221628605392414416)
XLA Ops:
  0.7 0.8 convert_multiply_fusion.1
  1.5 0.5 convert_reduce_fusion.1
  2.0 0.5 convert_reduce_fusion
  2.5 2.0 %fusion.25 = (bf16[133,1024]{1,0:T(8,128)(2,1)S(1)}, f32[133,1024]{1,0:T(8,128)S(1)}) fusion(bf16[1,1,133,1024]{3,2,1,0:T(8,128)(2,1)} %param.12, f32[1024]{0:T(1024)S(1)} %convert_reduce_fusion), kind=kOutput, calls=%fused_computation.60 | convolution fusion | flops 280105984 | bytes 1093632 | tf_op jit(solution)/shard_map/dot_general | solution.py:385
  4.5 0.1 fusion.20
  4.8 7.9 %collective-permute-start.1 = (bf16[144,1024]{1,0:T(8,128)(2,1)S(1)}, bf16[144,1024]{1,0:T(8,128)(2,1)S(1)}, u32[]{:S(2)}, u32[]{:S(2)}) collective-permute-start(bf16[144,1024]{1,0:T(8,128)(2,1)S(1)} %pad_maximum_fusion.1), channel_id=1, source_target_pairs={{4,0},{8,4},{12,8},{16,12},{20,16},{24,20},{28,24},{32,28},{36,32}... | collective-permute-start | bytes 884744 | tf_op jit(solution)/shard_map/ppermute | solution.py:372
  13.4 0.2 convert_reduce_fusion.3
  13.6 0.2 convert_reduce_fusion.2
  13.8 0.4 fusion.3
  14.2 0.2 copy.18.refs_2_
  14.9 3.4 %collective-permute-done.1 = bf16[144,1024]{1,0:T(8,128)(2,1)S(1)} collective-permute-done((bf16[144,1024]{1,0:T(8,128)(2,1)S(1)}, bf16[144,1024]{1,0:T(8,128)(2,1)S(1)}, u32[]{:S(2)}, u32[]{:S(2)}) %collective-permute-start.1) | collective-permute-done | bytes 294944 | tf_op jit(solution)/shard_map/ppermute | solution.py:372
  18.3 6.1 %collective-permute-done = bf16[144,1024]{1,0:T(8,128)(2,1)S(1)} collective-permute-done((bf16[144,1024]{1,0:T(8,128)(2,1)S(1)}, bf16[144,1024]{1,0:T(8,128)(2,1)S(1)}, u32[]{:S(2)}, u32[]{:S(2)}) %collective-permute-start) | collective-permute-done | bytes 294944 | tf_op jit(solution)/shard_map/ppermute | solution.py:372
  24.5 3.7 %collective-permute-start.3 = (bf16[3,144,1024]{2,1,0:T(8,128)(2,1)S(1)}, bf16[3,144,1024]{2,1,0:T(8,128)(2,1)S(1)}, u32[]{:S(2)}, u32[]{:S(2)}) collective-permute-start(bf16[3,144,1024]{2,1,0:T(8,128)(2,1)S(1)} %pad_maximum_fusion.refs_5_), channel_id=1, source_target_pairs={{1,0},{2,1},{3,2},{5,4},{6,5},{7,6},{9,8},{10,9},{11,10},{13,12},{... | collective-permute-start | bytes 2654216 | tf_op jit(solution)/shard_map/halo_dec/ppermute | solution.py:372
  28.3 4.5 %collective-permute-start.2 = (bf16[3,144,1024]{2,1,0:T(8,128)(2,1)S(1)}, bf16[3,144,1024]{2,1,0:T(8,128)(2,1)S(1)}, u32[]{:S(2)}, u32[]{:S(2)}) collective-permute-start(bf16[3,144,1024]{2,1,0:T(8,128)(2,1)S(1)} %pad_maximum_fusion.refs_5_), channel_id=1, source_target_pairs={{0,1},{1,2},{2,3},{4,5},{5,6},{6,7},{8,9},{9,10},{10,11},{12,13},{... | collective-permute-start | bytes 2654216 | tf_op jit(solution)/shard_map/halo_dec/ppermute | solution.py:372
  32.7 0.2 broadcast_in_dim.4.refs_3_
  33.0 9.6 %pairs_3.1.refs_7_ = f32[42,512,128]{2,1,0:T(8,128)S(1)} custom-call(s32[1]{0:T(128)} %bitcast.62.refs_0_, s32[2]{0:T(128)S(1)} %pad_add_fusion.refs_1_, f32[512,133]{1,0:T(8,128)S(1)} %copy.18.refs_2_, f32[2,512,128]{2,1,0:T(8,128)S(1)} %broadcast_in_dim.4.refs_3_, f32[8,128]{1,0:T(8,128)S(1)} %pad.8.refs_4_, bf16[3,144,1024]{2,1,0:T(8,128)(2,1)S(1)} %pad_maximum_fusion.refs_5_), custom_call_target="tpu_custom_call" | custom-call | flops 60000002048 | bytes 900000 | tf_op jit(solution)/shard_map/pairs_3/pallas_call | solution.py:303
  42.6 0.1 collective-permute-done.2.refs_5_
  42.7 10.5 %pairs_6.1.sums_ref = f32[512,128]{1,0:T(8,128)S(1)} custom-call(s32[1]{0:T(128)} %bitcast.63.refs_0_, s32[2]{0:T(128)S(1)} %pad_add_fusion.refs_1_, f32[512,133]{1,0:T(8,128)S(1)} %copy.18.refs_2_, f32[2,512,128]{2,1,0:T(8,128)S(1)} %broadcast_in_dim.4.refs_3_, f32[8,128]{1,0:T(8,128)S(1)} %pad.8.refs_4_, ...), custom_call_target="tpu_custom_call" | custom-call | flops 120000004096 | bytes 1800000 | tf_op jit(solution)/shard_map/pairs_6/pallas_call | solution.py:303
  53.3 2.2 %region_table.1 = f32[1024,384]{1,0:T(8,128)S(1)} custom-call(s32[1,512]{1,0:T(1,128)S(1)} %fusion.16.region_ref, s32[512,1]{1,0:T(8,128)S(1)} %slice_convert_fusion.sample_ref, f32[512,128]{1,0:T(8,128)S(1)} %pairs_6.1.sums_ref, bf16[128,384]{1,0:T(8,128)(2,1)S(1)} %copy-done), custom_call_target="tpu_custom_call" | custom-call | tf_op jit(solution)/shard_map/region_table/pallas_call | solution.py:356
  55.5 40.0 %all_to_all.9 = f32[128,8,384]{2,1,0:T(8,128)S(1)} all-to-all(f32[128,8,384]{2,1,0:T(8,128)S(1)} %bitcast.64), channel_id=1, replica_groups=mesh['ra'=32,'dec'=4] {'ra','dec'}, dimensions={0} | all-to-all | bytes 3145728 | tf_op jit(solution)/shard_map/all_to_all | solution.py:428
  95.6 0.2 reduce_sum.49
  95.7 0.1 reshape.363
  96.0 0.6 broadcast_multiply_fusion.1
  96.6 0.6 broadcast_multiply_fusion
  (40 shorter events, 0.8 us)
Async XLA Ops:
  0.6 12.7 %copy-start.3 = (s32[1,1,512]{2,1,0:T(1,128)S(1)}, s32[1,1,512]{2,1,0:T(1,128)}, u32[]{:S(2)}) copy-start(s32[1,1,512]{2,1,0:T(1,128)} %param.11) | copy-start | bytes 6148
  0.6 12.7 %copy-start.2 = (s32[1,1,512]{2,1,0:T(1,128)S(1)}, s32[1,1,512]{2,1,0:T(1,128)}, u32[]{:S(2)}) copy-start(s32[1,1,512]{2,1,0:T(1,128)} %param.10) | copy-start | bytes 6148
  0.6 12.7 %copy-start.6 = (bf16[1,1,130,512]{3,2,1,0:T(8,128)(2,1)S(1)}, bf16[1,1,130,512]{3,2,1,0:T(8,128)(2,1)}, u32[]{:S(2)}) copy-start(bf16[1,1,130,512]{3,2,1,0:T(8,128)(2,1)} %param.8) | copy-start | bytes 399364
  4.8 13.5 %collective-permute-start.1 = (bf16[144,1024]{1,0:T(8,128)(2,1)S(1)}, bf16[144,1024]{1,0:T(8,128)(2,1)S(1)}, u32[]{:S(2)}, u32[]{:S(2)}) collective-permute-start(bf16[144,1024]{1,0:T(8,128)(2,1)S(1)} %pad_maximum_fusion.1), channel_id=1, source_target_pairs={{4,0},{8,4},{12,8},{16,12},{20,16},{24,20},{28,24},{32,28},{36,32}... | collective-permute-start | bytes 884744 | tf_op jit(solution)/shard_map/ppermute | solution.py:372
  12.6 11.8 %collective-permute-start = (bf16[144,1024]{1,0:T(8,128)(2,1)S(1)}, bf16[144,1024]{1,0:T(8,128)(2,1)S(1)}, u32[]{:S(2)}, u32[]{:S(2)}) collective-permute-start(bf16[144,1024]{1,0:T(8,128)(2,1)S(1)} %pad_maximum_fusion.1), channel_id=1, source_target_pairs={{0,4},{4,8},{8,12},{12,16},{16,20},{20,24},{24,28},{28,32},{32,36}... | collective-permute-start | bytes 884744 | tf_op jit(solution)/shard_map/ppermute | solution.py:372
  24.5 18.0 %collective-permute-start.3 = (bf16[3,144,1024]{2,1,0:T(8,128)(2,1)S(1)}, bf16[3,144,1024]{2,1,0:T(8,128)(2,1)S(1)}, u32[]{:S(2)}, u32[]{:S(2)}) collective-permute-start(bf16[3,144,1024]{2,1,0:T(8,128)(2,1)S(1)} %pad_maximum_fusion.refs_5_), channel_id=1, source_target_pairs={{1,0},{2,1},{3,2},{5,4},{6,5},{7,6},{9,8},{10,9},{11,10},{13,12},{... | collective-permute-start | bytes 2654216 | tf_op jit(solution)/shard_map/halo_dec/ppermute | solution.py:372
  28.3 14.4 %collective-permute-start.2 = (bf16[3,144,1024]{2,1,0:T(8,128)(2,1)S(1)}, bf16[3,144,1024]{2,1,0:T(8,128)(2,1)S(1)}, u32[]{:S(2)}, u32[]{:S(2)}) collective-permute-start(bf16[3,144,1024]{2,1,0:T(8,128)(2,1)S(1)} %pad_maximum_fusion.refs_5_), channel_id=1, source_target_pairs={{0,1},{1,2},{2,3},{4,5},{5,6},{6,7},{8,9},{9,10},{10,11},{12,13},{... | collective-permute-start | bytes 2654216 | tf_op jit(solution)/shard_map/halo_dec/ppermute | solution.py:372
  32.9 9.8 %copy-start.1 = (bf16[5376,128]{1,0:T(8,128)(2,1)S(1)}, bf16[5376,128]{1,0:T(8,128)(2,1)}, u32[]{:S(2)}) copy-start(bf16[5376,128]{1,0:T(8,128)(2,1)} %constant.66.clone.refs_8_) | copy-start | bytes 4128772
  42.7 10.5 %copy-start = (bf16[128,384]{1,0:T(8,128)(2,1)S(1)}, bf16[128,384]{1,0:T(8,128)(2,1)}, u32[]{:S(2)}) copy-start(bf16[128,384]{1,0:T(8,128)(2,1)} %constant.67.clone.place_ref) | copy-start | bytes 294916
  55.5 40.4 %copy-start.5 = (f32[20]{0:T(128)S(1)}, f32[20]{0:T(128)}, u32[]{:S(2)}) copy-start(f32[20]{0:T(128)} %constant.78) | copy-start | bytes 244
  55.5 41.1 %copy-start.4 = (f32[20]{0:T(128)S(1)}, f32[20]{0:T(128)}, u32[]{:S(2)}) copy-start(f32[20]{0:T(128)} %constant.80) | copy-start | bytes 244

commit v3 on v2

--- a/solution.py
+++ b/solution.py
@@ -21,13 +21,14 @@
 SUB = 8
 SRC_TILES = S_PATCH // LANES
 LENS_TILES = L_PATCH // SUB
-UNROLL = (4, 4, 4)
+UNROLL = (4, 4, 8)
 CRIT_ROW = 5 * SUB
 FAR = 1.0e6
 BOX_ROW = ZROWS + SUB
 BLOCK_ROWS = 144
 LIST_WORDS = 16
-FOLD_SPLIT = 22
+LANE_SUMS = 18
+FOLD_SPLIT = 30
 VMEM_MIB = 26
 THRESHOLD_SUMS = 2 * (NBIN + 1)
 WIDE = 3 * LANES
@@ -212,11 +213,11 @@
                 before_ref[v, pl.ds(first, SUB), :] if later else jnp.zeros(tile_shape, jnp.float32)
             )
 
-        def far_step(i, word):
-            following = list_ref[i + 1, lens_tile]
+        def far_step(i, words):
+            following = (list_ref[2 * i + 2, lens_tile], list_ref[2 * i + 3, lens_tile])
             terms = []
-            for u in range(4):
-                tile = (word >> (7 * u)) & 127
+            for u in range(UNROLL[2]):
+                tile = (words[u // 4] >> (7 * (u % 4))) & 127
                 dx, dy = tables[tile, 0:SUB] - lens_x, tables[tile, SUB : 2 * SUB] - lens_y
                 dx_sq, dy_sq = dx * dx, dy * dy
                 r2 = dx_sq + dy_sq
@@ -232,7 +233,7 @@
             add_up(rows, terms, 2)
             return following
 
-        lax.fori_loop(0, trips[2], far_step, list_ref[0, lens_tile])
+        lax.fori_loop(0, trips[2], far_step, (list_ref[0, lens_tile], list_ref[1, lens_tile]))
         for group in (1, 0):
 
             def near_step(i, nothing, group=group):
@@ -258,16 +259,22 @@
         tiles_end = jnp.minimum(tiles_first + LANES // SUB, lens_tiles)
         lax.fori_loop(tiles_first, tiles_end, lens_step, first)
         high, low = [], []
-        for v in range(THRESHOLD_SUMS):
+        for v in range(LANE_SUMS, THRESHOLD_SUMS):
             value = sums[v]
             high.append(value.astype(jnp.bfloat16))
-            low.append((value - high[v].astype(jnp.float32)).astype(jnp.bfloat16))
+            low.append((value - high[-1].astype(jnp.float32)).astype(jnp.bfloat16))
         folded = []
-        for lo, hi in ((0, FOLD_SPLIT), (FOLD_SPLIT, THRESHOLD_SUMS)):
-            both = [jnp.concatenate(part[lo:hi], axis=1) for part in (high, low)]
+        for lo, hi in ((LANE_SUMS, FOLD_SPLIT), (FOLD_SPLIT, THRESHOLD_SUMS)):
+            both = [
+                jnp.concatenate(part[lo - LANE_SUMS : hi - LANE_SUMS], axis=1)
+                for part in (high, low)
+            ]
             weights = fold_ref[lo * LANES : hi * LANES, :]
             folded += [jnp.dot(p, weights, preferred_element_type=jnp.float32) for p in both]
         folded = tree_sum(folded)
+        lane = lax.broadcasted_iota(jnp.int32, (LANES, LANES), 1)
+        for v in range(LANE_SUMS):
+            folded = jnp.where(lane == v, jnp.sum(sums[v], axis=1, keepdims=True), folded)
         row = lax.broadcasted_iota(jnp.int32, (LANES, LANES), 0) + first
         folded = jnp.where(row < live, folded, 0.0)
         out_ref[pl.ds(first, LANES), :] = folded
@@ -337,10 +344,9 @@
 
 def table_kernel(region_ref, sample_ref, sums_ref, place_ref, out_ref):
     def product(matrices, others):
-        terms = [
-            jnp.dot(a, b, preferred_element_type=jnp.float32) for a, b in zip(matrices, others)
-        ]
-        return (terms[2] + terms[1]) + terms[0]
+        return tree_sum(
+            [jnp.dot(a, b, preferred_element_type=jnp.float32) for a, b in zip(matrices, others)][::-1]
+        )
 
     bins = product(split_parts(sums_ref[...]), [place_ref[...]] * 3)
     lane = lax.broadcasted_iota(jnp.int32, bins.shape, 1) - sample_ref[...] * (2 * NBIN)
@@ -348,7 +354,7 @@
     region = region_ref[...]
     ids = lax.broadcasted_iota(jnp.int32, (out_ref.shape[0], region.shape[1]), 0)
     match = (ids == region).astype(jnp.float32).astype(jnp.bfloat16)
-    out_ref[...] = product([match] * 3, split_parts(bins))
+    out_ref[...] = product([match] * 2, split_parts(bins)[:2])
 
 
 def region_sums(region, sample, sums, regions_total):

time: 98.4 us -> 97.1 us (0.987)
  Pallas kernels: 22.4 us -> 10.4 us
  blocking collectives: 40 us -> 45.8 us
  waiting for transfers between devices: 9.71 us -> 15.1 us
    pallas_call x2, Pallas kernels: 20.1 us -> 8.69 us  [pair_sums(): pl.pallas_call(functools.partial(pair_kernel, shifts, later, last), out_s...]
    all_to_all x1, blocking collectives: 40 us -> 45.8 us  [on_device(): table = lax.all_to_all(table, axes, 0, 0, tiled=True)]
    ppermute x2, waiting for transfers between devices: 3.44 us -> 7.73 us  [shifted(): lax.ppermute(block, axis, backward)]
    ppermute x2, waiting for transfers between devices: 6.27 us -> 7.32 us  [shifted(): lax.ppermute(block, axis, forward)]
  transfers between devices with their start and end apart: 4 -> 4, of which waited for: 3 -> 4; matrix products, arithmetic and copies ran while one was open for 2% -> 2% of each run, Pallas kernels for 10% -> 4%
where the time goes in v3:
time: 97.1 us; the launch traced here: 96.3 us
  blocking collectives  45.8 us (47%)
  starting transfers between devices  16 us (16%)
  waiting for transfers between devices  15.1 us (16%)
  Pallas kernels  10.4 us (11%)
  other arithmetic  4.2 us (4%)
  matrix products  2.39 us (2%)
  between operations  1.62 us (2%)
    all_to_all x1, blocking collectives, on_device(): table = lax.all_to_all(table, axes, 0, 0, tiled=True)  45.8 us
    ppermute x2, starting transfers between devices, shifted(): lax.ppermute(block, axis, backward)  11.6 us
    pallas_call x2, Pallas kernels, pair_sums(): pl.pallas_call(functools.partial(pair_kernel, shifts, later, last), out_s...  8.69 us
    ppermute x2, waiting for transfers between devices, shifted(): lax.ppermute(block, axis, backward)  7.73 us
    ppermute x2, waiting for transfers between devices, shifted(): lax.ppermute(block, axis, forward)  7.32 us
    ppermute x2, starting transfers between devices, shifted(): lax.ppermute(block, axis, forward)  4.48 us
    dot_general x1, matrix products, on_device(): lax.dot_general(source, order_matrix(source_rank), nothing, preferred_ele...  1.99 us
  transfers between devices with their start and end apart: 4, of which 4 were waited for; matrix products, arithmetic and copies ran while one was open for 2% of the time, Pallas kernels for 4%

profile of v3, /device:TPU:1, one launch (start us, length us, event | category | flops | bytes accessed | tf_op | source)
XLA Modules:
  0.0 96.3 jit_solution(17542037057265740232)
XLA Ops:
  0.7 0.8 convert_multiply_fusion.1
  1.5 0.5 convert_reduce_fusion.1
  2.0 0.5 convert_reduce_fusion
  2.5 2.0 %fusion.25 = (bf16[133,1024]{1,0:T(8,128)(2,1)S(1)}, f32[133,1024]{1,0:T(8,128)S(1)}) fusion(bf16[1,1,133,1024]{3,2,1,0:T(8,128)(2,1)} %param.12, f32[1024]{0:T(1024)S(1)} %convert_reduce_fusion), kind=kOutput, calls=%fused_computation.60 | convolution fusion | flops 280105984 | bytes 1093632 | tf_op jit(solution)/shard_map/dot_general | solution.py:391
  4.5 0.1 fusion.20
  4.8 7.9 %collective-permute-start.1 = (bf16[144,1024]{1,0:T(8,128)(2,1)S(1)}, bf16[144,1024]{1,0:T(8,128)(2,1)S(1)}, u32[]{:S(2)}, u32[]{:S(2)}) collective-permute-start(bf16[144,1024]{1,0:T(8,128)(2,1)S(1)} %pad_maximum_fusion.1), channel_id=1, source_target_pairs={{4,0},{8,4},{12,8},{16,12},{20,16},{24,20},{28,24},{32,28},{36,32}... | collective-permute-start | bytes 884744 | tf_op jit(solution)/shard_map/ppermute | solution.py:378
  13.4 0.2 convert_reduce_fusion.3
  13.6 0.2 convert_reduce_fusion.2
  13.8 0.4 fusion.3
  14.2 0.2 copy.18.refs_2_
  14.9 3.4 %collective-permute-done.1 = bf16[144,1024]{1,0:T(8,128)(2,1)S(1)} collective-permute-done((bf16[144,1024]{1,0:T(8,128)(2,1)S(1)}, bf16[144,1024]{1,0:T(8,128)(2,1)S(1)}, u32[]{:S(2)}, u32[]{:S(2)}) %collective-permute-start.1) | collective-permute-done | bytes 294944 | tf_op jit(solution)/shard_map/ppermute | solution.py:378
  18.3 6.1 %collective-permute-done = bf16[144,1024]{1,0:T(8,128)(2,1)S(1)} collective-permute-done((bf16[144,1024]{1,0:T(8,128)(2,1)S(1)}, bf16[144,1024]{1,0:T(8,128)(2,1)S(1)}, u32[]{:S(2)}, u32[]{:S(2)}) %collective-permute-start) | collective-permute-done | bytes 294944 | tf_op jit(solution)/shard_map/ppermute | solution.py:378
  24.5 3.7 %collective-permute-start.3 = (bf16[3,144,1024]{2,1,0:T(8,128)(2,1)S(1)}, bf16[3,144,1024]{2,1,0:T(8,128)(2,1)S(1)}, u32[]{:S(2)}, u32[]{:S(2)}) collective-permute-start(bf16[3,144,1024]{2,1,0:T(8,128)(2,1)S(1)} %pad_maximum_fusion.refs_5_), channel_id=1, source_target_pairs={{1,0},{2,1},{3,2},{5,4},{6,5},{7,6},{9,8},{10,9},{11,10},{13,12},{... | collective-permute-start | bytes 2654216 | tf_op jit(solution)/shard_map/halo_dec/ppermute | solution.py:378
  28.3 4.5 %collective-permute-start.2 = (bf16[3,144,1024]{2,1,0:T(8,128)(2,1)S(1)}, bf16[3,144,1024]{2,1,0:T(8,128)(2,1)S(1)}, u32[]{:S(2)}, u32[]{:S(2)}) collective-permute-start(bf16[3,144,1024]{2,1,0:T(8,128)(2,1)S(1)} %pad_maximum_fusion.refs_5_), channel_id=1, source_target_pairs={{0,1},{1,2},{2,3},{4,5},{5,6},{6,7},{8,9},{9,10},{10,11},{12,13},{... | collective-permute-start | bytes 2654216 | tf_op jit(solution)/shard_map/halo_dec/ppermute | solution.py:378
  32.7 0.2 broadcast_in_dim.4.refs_3_
  33.0 4.3 %pairs_3.1.refs_7_ = f32[42,512,128]{2,1,0:T(8,128)S(1)} custom-call(s32[1]{0:T(128)} %bitcast.62.refs_0_, s32[2]{0:T(128)S(1)} %pad_add_fusion.refs_1_, f32[512,133]{1,0:T(8,128)S(1)} %copy.18.refs_2_, f32[2,512,128]{2,1,0:T(8,128)S(1)} %broadcast_in_dim.4.refs_3_, f32[8,128]{1,0:T(8,128)S(1)} %pad.8.refs_4_, bf16[3,144,1024]{2,1,0:T(8,128)(2,1)S(1)} %pad_maximum_fusion.refs_5_), custom_call_target="tpu_custom_call" | custom-call | flops 60000002048 | bytes 900000 | tf_op jit(solution)/shard_map/pairs_3/pallas_call | solution.py:310
  37.2 4.3 %collective-permute-done.3.refs_6_ = bf16[3,144,1024]{2,1,0:T(8,128)(2,1)S(1)} collective-permute-done((bf16[3,144,1024]{2,1,0:T(8,128)(2,1)S(1)}, bf16[3,144,1024]{2,1,0:T(8,128)(2,1)S(1)}, u32[]{:S(2)}, u32[]{:S(2)}) %collective-permute-start.3) | collective-permute-done | bytes 884768 | tf_op jit(solution)/shard_map/halo_dec/ppermute | solution.py:378
  41.5 1.2 %collective-permute-done.2.refs_5_ = bf16[3,144,1024]{2,1,0:T(8,128)(2,1)S(1)} collective-permute-done((bf16[3,144,1024]{2,1,0:T(8,128)(2,1)S(1)}, bf16[3,144,1024]{2,1,0:T(8,128)(2,1)S(1)}, u32[]{:S(2)}, u32[]{:S(2)}) %collective-permute-start.2) | collective-permute-done | bytes 884768 | tf_op jit(solution)/shard_map/halo_dec/ppermute | solution.py:378
  42.7 4.4 %pairs_6.1.sums_ref = f32[512,128]{1,0:T(8,128)S(1)} custom-call(s32[1]{0:T(128)} %bitcast.63.refs_0_, s32[2]{0:T(128)S(1)} %pad_add_fusion.refs_1_, f32[512,133]{1,0:T(8,128)S(1)} %copy.18.refs_2_, f32[2,512,128]{2,1,0:T(8,128)S(1)} %broadcast_in_dim.4.refs_3_, f32[8,128]{1,0:T(8,128)S(1)} %pad.8.refs_4_, ...), custom_call_target="tpu_custom_call" | custom-call | flops 120000004096 | bytes 1800000 | tf_op jit(solution)/shard_map/pairs_6/pallas_call | solution.py:310
  47.2 1.7 %region_table.1 = f32[1024,384]{1,0:T(8,128)S(1)} custom-call(s32[1,512]{1,0:T(1,128)S(1)} %fusion.16.region_ref, s32[512,1]{1,0:T(8,128)S(1)} %slice_convert_fusion.sample_ref, f32[512,128]{1,0:T(8,128)S(1)} %pairs_6.1.sums_ref, bf16[128,384]{1,0:T(8,128)(2,1)S(1)} %copy-done), custom_call_target="tpu_custom_call" | custom-call | tf_op jit(solution)/shard_map/region_table/pallas_call | solution.py:362
  48.9 45.8 %all_to_all.9 = f32[128,8,384]{2,1,0:T(8,128)S(1)} all-to-all(f32[128,8,384]{2,1,0:T(8,128)S(1)} %bitcast.64), channel_id=1, replica_groups=mesh['ra'=32,'dec'=4] {'ra','dec'}, dimensions={0} | all-to-all | bytes 3145728 | tf_op jit(solution)/shard_map/all_to_all | solution.py:434
  94.7 0.2 reduce_sum.49
  95.1 0.6 broadcast_multiply_fusion.1
  95.7 0.6 broadcast_multiply_fusion
  (40 shorter events, 1.0 us)
Async XLA Ops:
  0.6 12.7 %copy-start.3 = (s32[1,1,512]{2,1,0:T(1,128)S(1)}, s32[1,1,512]{2,1,0:T(1,128)}, u32[]{:S(2)}) copy-start(s32[1,1,512]{2,1,0:T(1,128)} %param.11) | copy-start | bytes 6148
  0.6 12.7 %copy-start.2 = (s32[1,1,512]{2,1,0:T(1,128)S(1)}, s32[1,1,512]{2,1,0:T(1,128)}, u32[]{:S(2)}) copy-start(s32[1,1,512]{2,1,0:T(1,128)} %param.10) | copy-start | bytes 6148
  0.6 12.7 %copy-start.6 = (bf16[1,1,130,512]{3,2,1,0:T(8,128)(2,1)S(1)}, bf16[1,1,130,512]{3,2,1,0:T(8,128)(2,1)}, u32[]{:S(2)}) copy-start(bf16[1,1,130,512]{3,2,1,0:T(8,128)(2,1)} %param.8) | copy-start | bytes 399364
  4.8 13.5 %collective-permute-start.1 = (bf16[144,1024]{1,0:T(8,128)(2,1)S(1)}, bf16[144,1024]{1,0:T(8,128)(2,1)S(1)}, u32[]{:S(2)}, u32[]{:S(2)}) collective-permute-start(bf16[144,1024]{1,0:T(8,128)(2,1)S(1)} %pad_maximum_fusion.1), channel_id=1, source_target_pairs={{4,0},{8,4},{12,8},{16,12},{20,16},{24,20},{28,24},{32,28},{36,32}... | collective-permute-start | bytes 884744 | tf_op jit(solution)/shard_map/ppermute | solution.py:378
  12.6 11.8 %collective-permute-start = (bf16[144,1024]{1,0:T(8,128)(2,1)S(1)}, bf16[144,1024]{1,0:T(8,128)(2,1)S(1)}, u32[]{:S(2)}, u32[]{:S(2)}) collective-permute-start(bf16[144,1024]{1,0:T(8,128)(2,1)S(1)} %pad_maximum_fusion.1), channel_id=1, source_target_pairs={{0,4},{4,8},{8,12},{12,16},{16,20},{20,24},{24,28},{28,32},{32,36}... | collective-permute-start | bytes 884744 | tf_op jit(solution)/shard_map/ppermute | solution.py:378
  24.5 17.0 %collective-permute-start.3 = (bf16[3,144,1024]{2,1,0:T(8,128)(2,1)S(1)}, bf16[3,144,1024]{2,1,0:T(8,128)(2,1)S(1)}, u32[]{:S(2)}, u32[]{:S(2)}) collective-permute-start(bf16[3,144,1024]{2,1,0:T(8,128)(2,1)S(1)} %pad_maximum_fusion.refs_5_), channel_id=1, source_target_pairs={{1,0},{2,1},{3,2},{5,4},{6,5},{7,6},{9,8},{10,9},{11,10},{13,12},{... | collective-permute-start | bytes 2654216 | tf_op jit(solution)/shard_map/halo_dec/ppermute | solution.py:378
  28.3 14.4 %collective-permute-start.2 = (bf16[3,144,1024]{2,1,0:T(8,128)(2,1)S(1)}, bf16[3,144,1024]{2,1,0:T(8,128)(2,1)S(1)}, u32[]{:S(2)}, u32[]{:S(2)}) collective-permute-start(bf16[3,144,1024]{2,1,0:T(8,128)(2,1)S(1)} %pad_maximum_fusion.refs_5_), channel_id=1, source_target_pairs={{0,1},{1,2},{2,3},{4,5},{5,6},{6,7},{8,9},{9,10},{10,11},{12,13},{... | collective-permute-start | bytes 2654216 | tf_op jit(solution)/shard_map/halo_dec/ppermute | solution.py:378
  32.9 9.8 %copy-start.1 = (bf16[5376,128]{1,0:T(8,128)(2,1)S(1)}, bf16[5376,128]{1,0:T(8,128)(2,1)}, u32[]{:S(2)}) copy-start(bf16[5376,128]{1,0:T(8,128)(2,1)} %constant.66.clone.refs_8_) | copy-start | bytes 4128772
  42.7 4.4 %copy-start = (bf16[128,384]{1,0:T(8,128)(2,1)S(1)}, bf16[128,384]{1,0:T(8,128)(2,1)}, u32[]{:S(2)}) copy-start(bf16[128,384]{1,0:T(8,128)(2,1)} %constant.67.clone.place_ref) | copy-start | bytes 294916
  48.9 46.2 %copy-start.5 = (f32[20]{0:T(128)S(1)}, f32[20]{0:T(128)}, u32[]{:S(2)}) copy-start(f32[20]{0:T(128)} %constant.78) | copy-start | bytes 244
  48.9 46.8 %copy-start.4 = (f32[20]{0:T(128)S(1)}, f32[20]{0:T(128)}, u32[]{:S(2)}) copy-start(f32[20]{0:T(128)} %constant.80) | copy-start | bytes 244

commit v4 on v3

--- a/solution.py
+++ b/solution.py
@@ -46,13 +46,16 @@
 GROUPS = ((0, 10), (10, 16), (16, 21))
 
 
-def bin_scales():
+def lane_scales():
     lens_per_cell = L_PATCH / (SAMPLES * REG_DEV)
     density = S_PATCH / (PATCH * PATCH)
     expected = [
         math.pi * (EDGES[k + 1] - EDGES[k]) * density * lens_per_cell for k in range(NBIN)
     ]
-    return jnp.array(expected, jnp.float32)
+    expected = np.array(expected, np.float32)
+    row = np.ones((1, WIDE), np.float32)
+    row[0, : 2 * NBIN * SAMPLES] = np.tile(np.stack([np.sqrt(expected), expected]).ravel(), SAMPLES)
+    return jnp.asarray(row)
 
 
 def tree_sum(terms):
@@ -77,9 +80,57 @@
     return (target == rank[None, :]).astype(jnp.bfloat16)
 
 
-def tile_boxes(x, y):
-    x, y = x.reshape(-1, LANES), y.reshape(-1, LANES)
-    return jnp.stack([jnp.min(x, 1), jnp.max(x, 1), jnp.min(y, 1), jnp.max(y, 1)])
+def column_of(row):
+    return jnp.transpose(jnp.broadcast_to(row, (LANES, row.shape[1])))
+
+
+def row_ranks(row):
+    column = column_of(row)
+    ranks = []
+    for first in range(0, row.shape[1], LANES):
+        below = jnp.where(column < row[:, first : first + LANES], 1.0, 0.0)
+        ranks.append(jnp.sum(below, axis=0, keepdims=True))
+    return jnp.concatenate(ranks, axis=1)
+
+
+def source_kernel(source_ref, out_ref):
+    n = S_PATCH
+    index = lax.broadcasted_iota(jnp.int32, (1, n), 1).astype(jnp.float32)
+    place = source_ref[ZROWS : ZROWS + 2, :].astype(jnp.float32)
+    rank = row_ranks(place[0:1] * n + index)
+    key = jnp.floor(rank * (1.0 / 256)) * 2.0**18 + place[1:2] * n + index
+    rank = column_of(row_ranks(key))
+    lane = lax.broadcasted_iota(jnp.int32, (n, LANES), 1).astype(jnp.float32)
+    row = lax.broadcasted_iota(jnp.int32, (SRC_TILES, LANES), 0)
+    boxes = [jnp.zeros((SRC_TILES, LANES), jnp.float32) for _ in range(4)]
+    for first in range(0, n, 2 * LANES):
+        match = jnp.concatenate(
+            [jnp.where(rank == lane + float(first + at), 1.0, 0.0) for at in (0, LANES)], axis=1
+        )
+        ordered = jnp.dot(
+            source_ref[...], match.astype(jnp.bfloat16), preferred_element_type=jnp.float32
+        )
+        out_ref[: ZROWS + 5, first : first + 2 * LANES] = ordered.astype(jnp.bfloat16)
+        for at in (0, LANES):
+            for c in range(4):
+                values = ordered[ZROWS + c // 2 : ZROWS + c // 2 + 1, at : at + LANES]
+                reduce = jnp.max if c % 2 else jnp.min
+                bound = reduce(values, axis=1, keepdims=True)
+                boxes[c] = jnp.where(row == (first + at) // LANES, bound, boxes[c])
+    boxes = jnp.concatenate(boxes, axis=1).astype(jnp.bfloat16)
+    out_ref[BOX_ROW:, : 4 * LANES] = boxes
+
+
+def ordered_sources(source):
+    vmem = pl.BlockSpec(memory_space=pltpu.VMEM)
+    return pl.pallas_call(
+        source_kernel,
+        out_shape=jax.ShapeDtypeStruct((BLOCK_ROWS, S_PATCH), jnp.bfloat16),
+        in_specs=[vmem],
+        out_specs=vmem,
+        compiler_params=pltpu.CompilerParams(vmem_limit_bytes=VMEM_MIB << 20),
+        name="order_sources",
+    )(source)
 
 
 def tile_lists(lens_box, boxes, valid, tiles):
@@ -369,6 +420,27 @@
     )(region, sample, sums, bin_placement())
 
 
+def owned_kernel(parts_ref, scale_ref, signal_ref, weight_ref):
+    total = jnp.sum(parts_ref[...], axis=0) / scale_ref[...]
+    for m in range(SAMPLES):
+        for c, out_ref in enumerate((signal_ref, weight_ref)):
+            first = (2 * m + c) * NBIN
+            out_ref[:, m, :] = total[:, first : first + NBIN]
+
+
+def owned_sums(parts):
+    vmem = pl.BlockSpec(memory_space=pltpu.VMEM)
+    out = jax.ShapeDtypeStruct((REG_DEV, SAMPLES, NBIN), jnp.float32)
+    return pl.pallas_call(
+        owned_kernel,
+        out_shape=(out, out),
+        in_specs=[vmem] * 2,
+        out_specs=(vmem, vmem),
+        compiler_params=pltpu.CompilerParams(vmem_limit_bytes=VMEM_MIB << 20),
+        name="owned_sums",
+    )(parts, lane_scales())
+
+
 def shifted(block, axis, periodic):
     count = lax.axis_size(axis)
     forward = [(i, i + 1) for i in range(count - 1)]
@@ -384,18 +456,7 @@
     regions_total = REG_DEV * lax.axis_size("ra") * bands
     nothing = (((1,), (1,)), ((), ()))
 
-    source = source_block[0, 0]
-    source_rank = spatial_order(
-        source[ZROWS].astype(jnp.float32), source[ZROWS + 1].astype(jnp.float32), 0.0, 256
-    )
-    source = lax.dot_general(
-        source, order_matrix(source_rank), nothing, preferred_element_type=jnp.float32
-    )
-    boxes = tile_boxes(source[ZROWS], source[ZROWS + 1])
-    boxes = jnp.broadcast_to(boxes.T[:, :, None], (SRC_TILES, 4, LANES)).reshape(SRC_TILES, -1)
-    boxes = jnp.pad(boxes, ((BOX_ROW - ZROWS - 5, 0), (0, S_PATCH - 4 * LANES)))
-    source = jnp.concatenate([source, boxes], axis=0).astype(jnp.bfloat16)
-
+    source = ordered_sources(source_block[0, 0])
     low, high = shifted(source, "ra", True)
     middle = jnp.stack([source, low, high])
     columns_at = (0, -1, 1)
@@ -432,10 +493,7 @@
 
     table = region_sums(region, sample, sums, regions_total)
     table = lax.all_to_all(table, axes, 0, 0, tiled=True)
-    owned = jnp.sum(table.reshape(-1, REG_DEV, WIDE), axis=0)
-    owned = owned[:, : 2 * NBIN * SAMPLES].reshape(REG_DEV, SAMPLES, 2, NBIN)
-    scales = bin_scales()
-    return (owned[:, :, 0, :] / jnp.sqrt(scales), owned[:, :, 1, :] / scales)
+    return owned_sums(table.reshape(-1, REG_DEV, WIDE))
 
 
 def solution(mesh):

time: 97.1 us -> 95 us (0.978)
  Pallas kernels: 10.4 us -> 38.9 us
  blocking collectives: 45.8 us -> 25.9 us
  waiting for transfers between devices: 15.1 us -> 6.58 us
  other arithmetic: 4.2 us -> 2.99 us
  matrix products: 2.39 us -> 1.31 us
    pallas_call x2, Pallas kernels: 8.69 us -> 34.7 us  [pair_sums(): pl.pallas_call(functools.partial(pair_kernel, shifts, later, last), out_s...]
    all_to_all x1, blocking collectives: 45.8 us -> 25.9 us  [on_device(): table = lax.all_to_all(table, axes, 0, 0, tiled=True)]
    ppermute x2, waiting for transfers between devices: 7.73 us -> 0.44 us  [shifted(): lax.ppermute(block, axis, backward)]
    pallas_call x0 -> x2, Pallas kernels: none -> 2.51 us  [the longest x1 1.52 us: ordered_sources(): pl.pallas_call(source_kernel, out_shape=jax.ShapeDtypeStruct((BLOCK_ROWS,...]
    dot_general x1 -> x0, matrix products: 1.99 us -> none  [on_device(): lax.dot_general(source, order_matrix(source_rank), nothing, preferred_ele...]
    div x2 -> x0, other arithmetic: 1.24 us -> none  [on_device(): return (owned[:, :, 0, :] / jnp.sqrt(scales), owned[:, :, 1, :] / scales)]
    ppermute x2, waiting for transfers between devices: 7.32 us -> 6.14 us  [shifted(): lax.ppermute(block, axis, forward)]
  transfers between devices with their start and end apart: 4 -> 4, of which waited for: 4 -> 2; matrix products, arithmetic and copies ran while one was open for 2% -> 5% of each run, Pallas kernels for 4% -> 18%
where the time goes in v4:
time: 95 us; the launch traced here: 94.7 us
  Pallas kernels  38.9 us (41%)
  blocking collectives  25.9 us (27%)
  starting transfers between devices  16.1 us (17%)
  waiting for transfers between devices  6.58 us (7%)
  other arithmetic  2.99 us (3%)
  between operations  1.5 us (2%)
  local copies, waits for them, and re-layouts  1.46 us (2%)
  matrix products  1.31 us (1%)
    pallas_call x2, Pallas kernels, pair_sums(): pl.pallas_call(functools.partial(pair_kernel, shifts, later, last), out_s...  34.7 us
    all_to_all x1, blocking collectives, on_device(): table = lax.all_to_all(table, axes, 0, 0, tiled=True)  25.9 us
    ppermute x2, starting transfers between devices, shifted(): lax.ppermute(block, axis, backward)  11.6 us
    ppermute x2, waiting for transfers between devices, shifted(): lax.ppermute(block, axis, forward)  6.14 us
    ppermute x2, starting transfers between devices, shifted(): lax.ppermute(block, axis, forward)  4.48 us
  transfers between devices with their start and end apart: 4, of which 2 were waited for; matrix products, arithmetic and copies ran while one was open for 5% of the time, Pallas kernels for 18%

profile of v4, /device:TPU:1, one launch (start us, length us, event | category | flops | bytes accessed | tf_op | source)
XLA Modules:
  0.0 94.7 jit_solution(14775625565674549151)
XLA Ops:
  0.6 0.9 copy-done
  1.6 1.5 %order_sources.1 = bf16[144,1024]{1,0:T(8,128)(2,1)S(1)} custom-call(bf16[133,1024]{1,0:T(8,128)(2,1)S(1)} %bitcast.43), custom_call_target="tpu_custom_call" | custom-call | tf_op jit(solution)/shard_map/order_sources/pallas_call | solution.py:126
  3.1 7.8 %collective-permute-start.1 = (bf16[144,1024]{1,0:T(8,128)(2,1)S(1)}, bf16[144,1024]{1,0:T(8,128)(2,1)S(1)}, u32[]{:S(2)}, u32[]{:S(2)}) collective-permute-start(bf16[144,1024]{1,0:T(8,128)(2,1)S(1)} %order_sources.1), channel_id=1, source_target_pairs={{4,0},{8,4},{12,8},{16,12},{20,16},{24,20},{28,24},{32,28},{36,32}... | collective-permute-start | bytes 884744 | tf_op jit(solution)/shard_map/ppermute | solution.py:450
  11.6 0.7 convert_bitcast_fusion
  12.3 0.7 fusion.12
  13.0 0.8 convert_multiply_fusion.1
  13.8 0.2 convert_reduce_fusion.1
  14.0 0.2 convert_reduce_fusion
  14.2 1.3 %fusion = f32[512,133]{0,1:T(8,128)S(1)} fusion(f32[512]{0:T(512)S(1)} %convert_reduce_fusion, bf16[1,512]{1,0:T(2,128)(2,1)S(1)} %convert_bitcast_fusion, bf16[1,512]{1,0:T(2,128)(2,1)S(1)} %fusion.9, bf16[1,512]{1,0:T(2,128)(2,1)S(1)} %get-tuple-element.4, bf16[130,512]{1,0:T(8,128)(2,1)} %bitcast.51), kind=kOutput, calls=%fused_computation.3 | convolution fusion | flops 70537216 | bytes 410624 | tf_op jit(solution)/shard_map/dot_general | solution.py:476
  15.5 0.2 copy.18.refs_2_
  15.7 0.1 reshape.257
  15.8 0.1 fusion.14
  16.1 0.1 slice_convert_fusion.sample_ref
  16.2 0.4 collective-permute-done.1
  16.6 6.1 %collective-permute-done = bf16[144,1024]{1,0:T(8,128)(2,1)S(1)} collective-permute-done((bf16[144,1024]{1,0:T(8,128)(2,1)S(1)}, bf16[144,1024]{1,0:T(8,128)(2,1)S(1)}, u32[]{:S(2)}, u32[]{:S(2)}) %collective-permute-start) | collective-permute-done | bytes 294944 | tf_op jit(solution)/shard_map/ppermute | solution.py:450
  22.8 0.1 pad_maximum_fusion.refs_5_
  22.9 3.7 %collective-permute-start.3 = (bf16[3,144,1024]{2,1,0:T(8,128)(2,1)S(1)}, bf16[3,144,1024]{2,1,0:T(8,128)(2,1)S(1)}, u32[]{:S(2)}, u32[]{:S(2)}) collective-permute-start(bf16[3,144,1024]{2,1,0:T(8,128)(2,1)S(1)} %pad_maximum_fusion.refs_5_), channel_id=1, source_target_pairs={{1,0},{2,1},{3,2},{5,4},{6,5},{7,6},{9,8},{10,9},{11,10},{13,12},{... | collective-permute-start | bytes 2654216 | tf_op jit(solution)/shard_map/halo_dec/ppermute | solution.py:450
  26.6 4.5 %collective-permute-start.2 = (bf16[3,144,1024]{2,1,0:T(8,128)(2,1)S(1)}, bf16[3,144,1024]{2,1,0:T(8,128)(2,1)S(1)}, u32[]{:S(2)}, u32[]{:S(2)}) collective-permute-start(bf16[3,144,1024]{2,1,0:T(8,128)(2,1)S(1)} %pad_maximum_fusion.refs_5_), channel_id=1, source_target_pairs={{0,1},{1,2},{2,3},{4,5},{5,6},{6,7},{8,9},{9,10},{10,11},{12,13},{... | collective-permute-start | bytes 2654216 | tf_op jit(solution)/shard_map/halo_dec/ppermute | solution.py:450
  31.1 0.2 broadcast_in_dim.2.refs_3_
  31.3 16.6 %pairs_3.1.refs_7_ = f32[42,512,128]{2,1,0:T(8,128)S(1)} custom-call(s32[1]{0:T(128)} %bitcast.39.refs_0_, s32[2]{0:T(128)S(1)} %pad_add_fusion.refs_1_, f32[512,133]{1,0:T(8,128)S(1)} %copy.18.refs_2_, f32[2,512,128]{2,1,0:T(8,128)S(1)} %broadcast_in_dim.2.refs_3_, f32[8,128]{1,0:T(8,128)S(1)} %pad.4.refs_4_, bf16[3,144,1024]{2,1,0:T(8,128)(2,1)S(1)} %pad_maximum_fusion.refs_5_), custom_call_target="tpu_custom_call" | custom-call | flops 60000002048 | bytes 900000 | tf_op jit(solution)/shard_map/pairs_3/pallas_call | solution.py:361
  48.0 18.1 %pairs_6.1.sums_ref = f32[512,128]{1,0:T(8,128)S(1)} custom-call(s32[1]{0:T(128)} %bitcast.40.refs_0_, s32[2]{0:T(128)S(1)} %pad_add_fusion.refs_1_, f32[512,133]{1,0:T(8,128)S(1)} %copy.18.refs_2_, f32[2,512,128]{2,1,0:T(8,128)S(1)} %broadcast_in_dim.2.refs_3_, f32[8,128]{1,0:T(8,128)S(1)} %pad.4.refs_4_, ...), custom_call_target="tpu_custom_call" | custom-call | flops 120000004096 | bytes 1800000 | tf_op jit(solution)/shard_map/pairs_6/pallas_call | solution.py:361
  66.1 1.7 %region_table.1 = f32[1024,384]{1,0:T(8,128)S(1)} custom-call(s32[1,512]{1,0:T(1,128)S(1)} %fusion.11.region_ref, s32[512,1]{1,0:T(8,128)S(1)} %slice_convert_fusion.sample_ref, f32[512,128]{1,0:T(8,128)S(1)} %pairs_6.1.sums_ref, bf16[128,384]{1,0:T(8,128)(2,1)S(1)} %copy-done.1), custom_call_target="tpu_custom_call" | custom-call | tf_op jit(solution)/shard_map/region_table/pallas_call | solution.py:413
  67.8 25.9 %all_to_all.9.parts_ref = f32[128,8,384]{2,1,0:T(8,128)S(1)} all-to-all(f32[128,8,384]{2,1,0:T(8,128)S(1)} %bitcast.41), channel_id=1, replica_groups=mesh['ra'=32,'dec'=4] {'ra','dec'}, dimensions={0} | all-to-all | bytes 3145728 | tf_op jit(solution)/shard_map/all_to_all | solution.py:495
  93.7 1.0 %owned_sums.1 = (f32[8,8,20]{2,1,0:T(8,128)}, f32[8,8,20]{2,1,0:T(8,128)}) custom-call(f32[128,8,384]{2,1,0:T(8,128)S(1)} %all_to_all.9.parts_ref, f32[1,384]{1,0:T(1,128)S(1)} %copy-done.2), custom_call_target="tpu_custom_call" | custom-call | tf_op jit(solution)/shard_map/owned_sums/pallas_call | solution.py:434
  (19 shorter events, 0.2 us)
Async XLA Ops:
  0.6 1.0 %copy-start = (bf16[1,1,133,1024]{3,2,1,0:T(8,128)(2,1)S(1)}, bf16[1,1,133,1024]{3,2,1,0:T(8,128)(2,1)}, u32[]{:S(2)}) copy-start(bf16[1,1,133,1024]{3,2,1,0:T(8,128)(2,1)} %param.12) | copy-start | bytes 817156
  3.1 13.5 %collective-permute-start.1 = (bf16[144,1024]{1,0:T(8,128)(2,1)S(1)}, bf16[144,1024]{1,0:T(8,128)(2,1)S(1)}, u32[]{:S(2)}, u32[]{:S(2)}) collective-permute-start(bf16[144,1024]{1,0:T(8,128)(2,1)S(1)} %order_sources.1), channel_id=1, source_target_pairs={{4,0},{8,4},{12,8},{16,12},{20,16},{24,20},{28,24},{32,28},{36,32}... | collective-permute-start | bytes 884744 | tf_op jit(solution)/shard_map/ppermute | solution.py:450
  11.0 11.8 %collective-permute-start = (bf16[144,1024]{1,0:T(8,128)(2,1)S(1)}, bf16[144,1024]{1,0:T(8,128)(2,1)S(1)}, u32[]{:S(2)}, u32[]{:S(2)}) collective-permute-start(bf16[144,1024]{1,0:T(8,128)(2,1)S(1)} %order_sources.1), channel_id=1, source_target_pairs={{0,4},{4,8},{8,12},{12,16},{16,20},{20,24},{24,28},{28,32},{32,36}... | collective-permute-start | bytes 884744 | tf_op jit(solution)/shard_map/ppermute | solution.py:450
  22.9 25.1 %collective-permute-start.3 = (bf16[3,144,1024]{2,1,0:T(8,128)(2,1)S(1)}, bf16[3,144,1024]{2,1,0:T(8,128)(2,1)S(1)}, u32[]{:S(2)}, u32[]{:S(2)}) collective-permute-start(bf16[3,144,1024]{2,1,0:T(8,128)(2,1)S(1)} %pad_maximum_fusion.refs_5_), channel_id=1, source_target_pairs={{1,0},{2,1},{3,2},{5,4},{6,5},{7,6},{9,8},{10,9},{11,10},{13,12},{... | collective-permute-start | bytes 2654216 | tf_op jit(solution)/shard_map/halo_dec/ppermute | solution.py:450
  26.6 21.3 %collective-permute-start.2 = (bf16[3,144,1024]{2,1,0:T(8,128)(2,1)S(1)}, bf16[3,144,1024]{2,1,0:T(8,128)(2,1)S(1)}, u32[]{:S(2)}, u32[]{:S(2)}) collective-permute-start(bf16[3,144,1024]{2,1,0:T(8,128)(2,1)S(1)} %pad_maximum_fusion.refs_5_), channel_id=1, source_target_pairs={{0,1},{1,2},{2,3},{4,5},{5,6},{6,7},{8,9},{9,10},{10,11},{12,13},{... | collective-permute-start | bytes 2654216 | tf_op jit(solution)/shard_map/halo_dec/ppermute | solution.py:450
  31.3 16.6 %copy-start.3 = (bf16[5376,128]{1,0:T(8,128)(2,1)S(1)}, bf16[5376,128]{1,0:T(8,128)(2,1)}, u32[]{:S(2)}) copy-start(bf16[5376,128]{1,0:T(8,128)(2,1)} %constant.60.clone.refs_8_) | copy-start | bytes 4128772
  48.0 18.2 %copy-start.1 = (bf16[128,384]{1,0:T(8,128)(2,1)S(1)}, bf16[128,384]{1,0:T(8,128)(2,1)}, u32[]{:S(2)}) copy-start(bf16[128,384]{1,0:T(8,128)(2,1)} %constant.61.clone.place_ref) | copy-start | bytes 294916
  67.8 25.9 %copy-start.2 = (f32[1,384]{1,0:T(1,128)S(1)}, f32[1,384]{1,0:T(1,128)}, u32[]{:S(2)}) copy-start(f32[1,384]{1,0:T(1,128)} %constant.62.clone.scale_ref) | copy-start | bytes 4612

commit v5 on v4

--- a/solution.py
+++ b/solution.py
@@ -27,8 +27,8 @@
 BOX_ROW = ZROWS + SUB
 BLOCK_ROWS = 144
 LIST_WORDS = 16
-LANE_SUMS = 18
-FOLD_SPLIT = 30
+LANE_SUMS = 22
+FOLD_SPLIT = 32
 VMEM_MIB = 26
 THRESHOLD_SUMS = 2 * (NBIN + 1)
 WIDE = 3 * LANES
@@ -43,7 +43,7 @@
 
 
 EDGES = edge_squares()
-GROUPS = ((0, 10), (10, 16), (16, 21))
+GROUPS = ((1, 10), (10, 16), (16, 21))
 
 
 def lane_scales():
@@ -272,10 +272,11 @@
                 dx, dy = tables[tile, 0:SUB] - lens_x, tables[tile, SUB : 2 * SUB] - lens_y
                 dx_sq, dy_sq = dx * dx, dy * dy
                 r2 = dx_sq + dy_sq
+                r2 = jnp.where(r2 >= EDGES[0], r2, FAR)
                 turned = tables[tile, 2 * SUB : 3 * SUB] * (dx_sq - dy_sq)
                 turned = turned + tables[tile, 3 * SUB : 4 * SUB] * (dx * dy)
                 value = tables[tile, pl.ds(CRIT_ROW + first, SUB), :]
-                signal = value * (turned / jnp.maximum(r2, EDGES[0]))
+                signal = value * (turned / r2)
                 weight = tables[tile, 4 * SUB : 5 * SUB] * value * value
                 slots[0, i * UNROLL[2] + u] = signal
                 slots[1, i * UNROLL[2] + u] = weight

time: 95 us -> 93.5 us (0.984); the launches traced: 94.7 us -> 94.3 us
  transfers between devices with their start and end apart: 4 -> 4, of which waited for: 2 -> 2; matrix products, arithmetic and copies ran while one was open for 5% -> 5% of each run, Pallas kernels for 18% -> 17%
where the time goes in v5:
time: 93.5 us; the launch traced here: 94.3 us
  Pallas kernels  38.6 us (41%)
  blocking collectives  25.9 us (28%)
  starting transfers between devices  16.1 us (17%)
  waiting for transfers between devices  6.58 us (7%)
  other arithmetic  2.99 us (3%)
  between operations  1.5 us (2%)
  local copies, waits for them, and re-layouts  1.46 us (2%)
  matrix products  1.31 us (1%)
    pallas_call x2, Pallas kernels, pair_sums(): pl.pallas_call(functools.partial(pair_kernel, shifts, later, last), out_s...  34.4 us
    all_to_all x1, blocking collectives, on_device(): table = lax.all_to_all(table, axes, 0, 0, tiled=True)  25.9 us
    ppermute x2, starting transfers between devices, shifted(): lax.ppermute(block, axis, backward)  11.6 us
    ppermute x2, waiting for transfers between devices, shifted(): lax.ppermute(block, axis, forward)  6.14 us
    ppermute x2, starting transfers between devices, shifted(): lax.ppermute(block, axis, forward)  4.48 us
  transfers between devices with their start and end apart: 4, of which 2 were waited for; matrix products, arithmetic and copies ran while one was open for 5% of the time, Pallas kernels for 17%

profile of v5, /device:TPU:1, one launch (start us, length us, event | category | flops | bytes accessed | tf_op | source)
XLA Modules:
  0.0 94.3 jit_solution(9994987396086575428)
XLA Ops:
  0.6 0.9 %copy-done = bf16[1,1,133,1024]{3,2,1,0:T(8,128)(2,1)S(1)} copy-done((bf16[1,1,133,1024]{3,2,1,0:T(8,128)(2,1)S(1)}, bf16[1,1,133,1024]{3,2,1,0:T(8,128)(2,1)}, u32[]{:S(2)}) %copy-start) | copy-done | bytes 272408
  1.6 1.5 %order_sources.1 = bf16[144,1024]{1,0:T(8,128)(2,1)S(1)} custom-call(bf16[133,1024]{1,0:T(8,128)(2,1)S(1)} %bitcast.43), custom_call_target="tpu_custom_call" | custom-call | tf_op jit(solution)/shard_map/order_sources/pallas_call | solution.py:126
  3.1 7.8 %collective-permute-start.1 = (bf16[144,1024]{1,0:T(8,128)(2,1)S(1)}, bf16[144,1024]{1,0:T(8,128)(2,1)S(1)}, u32[]{:S(2)}, u32[]{:S(2)}) collective-permute-start(bf16[144,1024]{1,0:T(8,128)(2,1)S(1)} %order_sources.1), channel_id=1, source_target_pairs={{4,0},{8,4},{12,8},{16,12},{20,16},{24,20},{28,24},{32,28},{36,32}... | collective-permute-start | bytes 884744 | tf_op jit(solution)/shard_map/ppermute | solution.py:451
  11.6 0.7 convert_bitcast_fusion
  12.3 0.7 fusion.12
  13.0 0.8 convert_multiply_fusion.1
  13.8 0.2 convert_reduce_fusion.1
  14.0 0.2 convert_reduce_fusion
  14.2 1.3 %fusion = f32[512,133]{0,1:T(8,128)S(1)} fusion(f32[512]{0:T(512)S(1)} %convert_reduce_fusion, bf16[1,512]{1,0:T(2,128)(2,1)S(1)} %convert_bitcast_fusion, bf16[1,512]{1,0:T(2,128)(2,1)S(1)} %fusion.9, bf16[1,512]{1,0:T(2,128)(2,1)S(1)} %get-tuple-element.4, bf16[130,512]{1,0:T(8,128)(2,1)} %bitcast.51), kind=kOutput, calls=%fused_computation.3 | convolution fusion | flops 70537216 | bytes 410624 | tf_op jit(solution)/shard_map/dot_general | solution.py:477
  15.5 0.2 copy.18.refs_2_
  15.7 0.1 reshape.257
  15.8 0.1 fusion.14
  16.1 0.1 slice_convert_fusion.sample_ref
  16.2 0.4 collective-permute-done.1
  16.6 6.1 %collective-permute-done = bf16[144,1024]{1,0:T(8,128)(2,1)S(1)} collective-permute-done((bf16[144,1024]{1,0:T(8,128)(2,1)S(1)}, bf16[144,1024]{1,0:T(8,128)(2,1)S(1)}, u32[]{:S(2)}, u32[]{:S(2)}) %collective-permute-start) | collective-permute-done | bytes 294944 | tf_op jit(solution)/shard_map/ppermute | solution.py:451
  22.8 0.1 pad_maximum_fusion.refs_5_
  22.9 3.7 %collective-permute-start.3 = (bf16[3,144,1024]{2,1,0:T(8,128)(2,1)S(1)}, bf16[3,144,1024]{2,1,0:T(8,128)(2,1)S(1)}, u32[]{:S(2)}, u32[]{:S(2)}) collective-permute-start(bf16[3,144,1024]{2,1,0:T(8,128)(2,1)S(1)} %pad_maximum_fusion.refs_5_), channel_id=1, source_target_pairs={{1,0},{2,1},{3,2},{5,4},{6,5},{7,6},{9,8},{10,9},{11,10},{13,12},{... | collective-permute-start | bytes 2654216 | tf_op jit(solution)/shard_map/halo_dec/ppermute | solution.py:451
  26.6 4.5 %collective-permute-start.2 = (bf16[3,144,1024]{2,1,0:T(8,128)(2,1)S(1)}, bf16[3,144,1024]{2,1,0:T(8,128)(2,1)S(1)}, u32[]{:S(2)}, u32[]{:S(2)}) collective-permute-start(bf16[3,144,1024]{2,1,0:T(8,128)(2,1)S(1)} %pad_maximum_fusion.refs_5_), channel_id=1, source_target_pairs={{0,1},{1,2},{2,3},{4,5},{5,6},{6,7},{8,9},{9,10},{10,11},{12,13},{... | collective-permute-start | bytes 2654216 | tf_op jit(solution)/shard_map/halo_dec/ppermute | solution.py:451
  31.1 0.2 broadcast_in_dim.2.refs_3_
  31.3 16.4 %pairs_3.1.refs_7_ = f32[42,512,128]{2,1,0:T(8,128)S(1)} custom-call(s32[1]{0:T(128)} %bitcast.39.refs_0_, s32[2]{0:T(128)S(1)} %pad_add_fusion.refs_1_, f32[512,133]{1,0:T(8,128)S(1)} %copy.18.refs_2_, f32[2,512,128]{2,1,0:T(8,128)S(1)} %broadcast_in_dim.2.refs_3_, f32[8,128]{1,0:T(8,128)S(1)} %pad.4.refs_4_, bf16[3,144,1024]{2,1,0:T(8,128)(2,1)S(1)} %pad_maximum_fusion.refs_5_), custom_call_target="tpu_custom_call" | custom-call | flops 60000002048 | bytes 900000 | tf_op jit(solution)/shard_map/pairs_3/pallas_call | solution.py:362
  47.7 18.0 %pairs_6.1.sums_ref = f32[512,128]{1,0:T(8,128)S(1)} custom-call(s32[1]{0:T(128)} %bitcast.40.refs_0_, s32[2]{0:T(128)S(1)} %pad_add_fusion.refs_1_, f32[512,133]{1,0:T(8,128)S(1)} %copy.18.refs_2_, f32[2,512,128]{2,1,0:T(8,128)S(1)} %broadcast_in_dim.2.refs_3_, f32[8,128]{1,0:T(8,128)S(1)} %pad.4.refs_4_, ...), custom_call_target="tpu_custom_call" | custom-call | flops 120000004096 | bytes 1800000 | tf_op jit(solution)/shard_map/pairs_6/pallas_call | solution.py:362
  65.8 1.7 %region_table.1 = f32[1024,384]{1,0:T(8,128)S(1)} custom-call(s32[1,512]{1,0:T(1,128)S(1)} %fusion.11.region_ref, s32[512,1]{1,0:T(8,128)S(1)} %slice_convert_fusion.sample_ref, f32[512,128]{1,0:T(8,128)S(1)} %pairs_6.1.sums_ref, bf16[128,384]{1,0:T(8,128)(2,1)S(1)} %copy-done.1), custom_call_target="tpu_custom_call" | custom-call | tf_op jit(solution)/shard_map/region_table/pallas_call | solution.py:414
  67.5 25.9 %all_to_all.9.parts_ref = f32[128,8,384]{2,1,0:T(8,128)S(1)} all-to-all(f32[128,8,384]{2,1,0:T(8,128)S(1)} %bitcast.41), channel_id=1, replica_groups=mesh['ra'=32,'dec'=4] {'ra','dec'}, dimensions={0} | all-to-all | bytes 3145728 | tf_op jit(solution)/shard_map/all_to_all | solution.py:496
  93.3 1.0 %owned_sums.1 = (f32[8,8,20]{2,1,0:T(8,128)}, f32[8,8,20]{2,1,0:T(8,128)}) custom-call(f32[128,8,384]{2,1,0:T(8,128)S(1)} %all_to_all.9.parts_ref, f32[1,384]{1,0:T(1,128)S(1)} %copy-done.2), custom_call_target="tpu_custom_call" | custom-call | tf_op jit(solution)/shard_map/owned_sums/pallas_call | solution.py:435
  (19 shorter events, 0.2 us)
Async XLA Ops:
  0.6 1.0 %copy-start = (bf16[1,1,133,1024]{3,2,1,0:T(8,128)(2,1)S(1)}, bf16[1,1,133,1024]{3,2,1,0:T(8,128)(2,1)}, u32[]{:S(2)}) copy-start(bf16[1,1,133,1024]{3,2,1,0:T(8,128)(2,1)} %param.12) | copy-start | bytes 817156
  3.1 13.5 %collective-permute-start.1 = (bf16[144,1024]{1,0:T(8,128)(2,1)S(1)}, bf16[144,1024]{1,0:T(8,128)(2,1)S(1)}, u32[]{:S(2)}, u32[]{:S(2)}) collective-permute-start(bf16[144,1024]{1,0:T(8,128)(2,1)S(1)} %order_sources.1), channel_id=1, source_target_pairs={{4,0},{8,4},{12,8},{16,12},{20,16},{24,20},{28,24},{32,28},{36,32}... | collective-permute-start | bytes 884744 | tf_op jit(solution)/shard_map/ppermute | solution.py:451
  11.0 11.8 %collective-permute-start = (bf16[144,1024]{1,0:T(8,128)(2,1)S(1)}, bf16[144,1024]{1,0:T(8,128)(2,1)S(1)}, u32[]{:S(2)}, u32[]{:S(2)}) collective-permute-start(bf16[144,1024]{1,0:T(8,128)(2,1)S(1)} %order_sources.1), channel_id=1, source_target_pairs={{0,4},{4,8},{8,12},{12,16},{16,20},{20,24},{24,28},{28,32},{32,36}... | collective-permute-start | bytes 884744 | tf_op jit(solution)/shard_map/ppermute | solution.py:451
  22.9 24.8 %collective-permute-start.3 = (bf16[3,144,1024]{2,1,0:T(8,128)(2,1)S(1)}, bf16[3,144,1024]{2,1,0:T(8,128)(2,1)S(1)}, u32[]{:S(2)}, u32[]{:S(2)}) collective-permute-start(bf16[3,144,1024]{2,1,0:T(8,128)(2,1)S(1)} %pad_maximum_fusion.refs_5_), channel_id=1, source_target_pairs={{1,0},{2,1},{3,2},{5,4},{6,5},{7,6},{9,8},{10,9},{11,10},{13,12},{... | collective-permute-start | bytes 2654216 | tf_op jit(solution)/shard_map/halo_dec/ppermute | solution.py:451
  26.6 21.1 %collective-permute-start.2 = (bf16[3,144,1024]{2,1,0:T(8,128)(2,1)S(1)}, bf16[3,144,1024]{2,1,0:T(8,128)(2,1)S(1)}, u32[]{:S(2)}, u32[]{:S(2)}) collective-permute-start(bf16[3,144,1024]{2,1,0:T(8,128)(2,1)S(1)} %pad_maximum_fusion.refs_5_), channel_id=1, source_target_pairs={{0,1},{1,2},{2,3},{4,5},{5,6},{6,7},{8,9},{9,10},{10,11},{12,13},{... | collective-permute-start | bytes 2654216 | tf_op jit(solution)/shard_map/halo_dec/ppermute | solution.py:451
  31.3 16.4 %copy-start.3 = (bf16[5376,128]{1,0:T(8,128)(2,1)S(1)}, bf16[5376,128]{1,0:T(8,128)(2,1)}, u32[]{:S(2)}) copy-start(bf16[5376,128]{1,0:T(8,128)(2,1)} %constant.60.clone.refs_8_) | copy-start | bytes 4128772
  47.7 18.0 %copy-start.1 = (bf16[128,384]{1,0:T(8,128)(2,1)S(1)}, bf16[128,384]{1,0:T(8,128)(2,1)}, u32[]{:S(2)}) copy-start(bf16[128,384]{1,0:T(8,128)(2,1)} %constant.61.clone.place_ref) | copy-start | bytes 294916
  67.5 25.9 %copy-start.2 = (f32[1,384]{1,0:T(1,128)S(1)}, f32[1,384]{1,0:T(1,128)}, u32[]{:S(2)}) copy-start(f32[1,384]{1,0:T(1,128)} %constant.62.clone.scale_ref) | copy-start | bytes 4612
